TPU v7x, 1024 devices: a whole 4x8x16 slice. The times are simulated.
1024 devices in a mesh: dom: 2 (over core), gx: 32 (over y, z_hi), gy: 16 (over z_lo, x).
Axes of the slice: x: 4, y: 8, z: 16 (z_hi: 4, z_lo: 4; z = z_hi * 4 + z_lo), core: 2. Of those that a mesh axis runs over, the one named last changes fastest.
Arguments:
- wind: float32 [2, 3, 512, 256, 128], P('dom', None, 'gx', 'gy'), may hold values from -6 to 6
- adjoint: float32 [2, 4, 512, 256, 128], P('dom', None, 'gx', 'gy'), may hold values from -6 to 6
- turbines: int32 [512, 256, 128], P('gx', 'gy'), may hold values 0 or 1
- fringe_range: int32 [2], replicated, may hold values from 64 to 511, as said below
Outputs:
- earlier: float32 [2, 4, 512, 256, 128], P('dom', None, 'gx', 'gy')
Inputs may be any that keep to these rules, and one draw needn't show every extreme that they name: `fringe_range`: element 0 is the first streamwise cell of the fringe, the last cell 512 - 1 of the domain, and element 1 its length in cells, from 64 to 128; the fringe wraps around the periodic streamwise dimension.
All inputs are finite; a program needn't handle non-finite values. No bound on the sum of `turbines` on one device may be relied on, other than what follows from the above.
Results may differ from a plain program's by a relative error of at most 0.00002.
Values sent between devices are 32-bit elements; how exact they have to be, the bound alone decides.
No kernel may reach another device: no remote copies, remote signals or barrier semaphores. Data moves between devices by JAX's collectives and lax.ppermute only.
A program may use at most 32 MiB of HBM per device.

v0:
```python
import math

import jax
import jax.numpy as jnp
from jax import lax
from jax.sharding import PartitionSpec as P

DT = 0.1
SMAG = 0.1
SOUND_SQ = 4.0
DRAG = 1.0
RATE = 3.0


def padded_2(shard, sides, width):
    for axis, dim in sides:
        devices, length = (lax.axis_size(axis), shard.shape[dim])
        up = [(i, (i + 1) % devices) for i in range(devices)]
        down = [(j, i) for i, j in up]
        last = lax.slice_in_dim(shard, length - width, length, axis=dim)
        leading = lax.slice_in_dim(shard, 0, width, axis=dim)
        before = lax.ppermute(last, axis, up)
        after = lax.ppermute(leading, axis, down)
        shard = jnp.concatenate([before, shard, after], axis=dim)
    return shard


def passed_along(shard, axis, by):
    devices = lax.axis_size(axis)
    pairs = [(i, i + by) for i in range(devices) if 0 <= i + by < devices]
    return lax.ppermute(shard, axis, pairs)


def crop_xy(field, margin):
    if margin == 0:
        return field
    return field[..., margin : field.shape[-3] - margin, margin : field.shape[-2] - margin, :]


def pad_z(field):
    return jnp.pad(field, [(0, 0)] * (field.ndim - 1) + [(1, 1)])


def diff_x(field):
    return 0.5 * (field[..., 2:, 1:-1, :] - field[..., :-2, 1:-1, :])


def diff_y(field):
    return 0.5 * (field[..., 1:-1, 2:, :] - field[..., 1:-1, :-2, :])


def diff_z(field):
    padded = crop_xy(pad_z(field), 1)
    return 0.5 * (padded[..., 2:] - padded[..., :-2])


def eddy(wind_ext):
    grads = (diff_x(wind_ext), diff_y(wind_ext), diff_z(wind_ext))
    strain_sq = jnp.zeros_like(grads[0][0])
    for first in range(3):
        for second in range(3):
            strain = 0.5 * (grads[first][second] + grads[second][first])
            strain_sq = strain_sq + strain * strain
    return SMAG * jnp.sqrt(2.0 * strain_sq)


def spread(field, viscosity):
    centre = crop_xy(field, 1)
    visc_mid = crop_xy(viscosity, 1)
    flux_xp = (viscosity[..., 2:, 1:-1, :] + visc_mid) * 0.5 * (field[..., 2:, 1:-1, :] - centre)
    flux_xm = (visc_mid + viscosity[..., :-2, 1:-1, :]) * 0.5 * (centre - field[..., :-2, 1:-1, :])
    flux_yp = (viscosity[..., 1:-1, 2:, :] + visc_mid) * 0.5 * (field[..., 1:-1, 2:, :] - centre)
    flux_ym = (visc_mid + viscosity[..., 1:-1, :-2, :]) * 0.5 * (centre - field[..., 1:-1, :-2, :])
    visc_pad = pad_z(visc_mid)
    field_pad = pad_z(centre)
    flux_zp = (visc_pad[..., 2:] + visc_mid) * 0.5 * (field_pad[..., 2:] - centre)
    flux_zm = (visc_mid + visc_pad[..., :-2]) * 0.5 * (centre - field_pad[..., :-2])
    return flux_xp - flux_xm + flux_yp - flux_ym + flux_zp - flux_zm


def tendency(adjoint_ext, wind_here, viscosity, drag_cells):
    along_x = diff_x(adjoint_ext)
    along_y = diff_y(adjoint_ext)
    along_z = diff_z(adjoint_ext)
    advection = wind_here[0] * along_x + wind_here[1] * along_y + wind_here[2] * along_z
    diffusion = spread(adjoint_ext[:3], viscosity)
    wind_speed = jnp.sqrt(
        wind_here[0] * wind_here[0] + wind_here[1] * wind_here[1] + wind_here[2] * wind_here[2]
    )
    centre = crop_xy(adjoint_ext, 1)
    acoustic = SOUND_SQ * jnp.stack([along_x[3], along_y[3], along_z[3]], 0)
    velocity = advection[:3] + diffusion + acoustic - DRAG * drag_cells * wind_speed * centre[:3]
    pressure = advection[3] + along_x[0] + along_y[1] + along_z[2]
    return (centre, jnp.concatenate([velocity, pressure[None]], 0))


def ramp(position, fringe_range, length_total):
    offset = jnp.mod(position - fringe_range[0], length_total)
    fringe_width = fringe_range[1]
    fringe_phase = math.pi * (offset.astype(jnp.float32) + 0.5) / fringe_width.astype(jnp.float32)
    sine = jnp.sin(fringe_phase)
    return jnp.where(offset < fringe_width, RATE * sine * sine, 0.0)


def on_device(wind, adjoint, turbines, fringe_range):
    is_main = lax.axis_index("dom") == 0
    cells_x = wind.shape[2]
    length_total = cells_x * lax.axis_size("gx")
    anchor = lax.axis_index("gx") * cells_x
    background = jnp.concatenate([wind[0], turbines[None].astype(jnp.float32)], 0)
    reach = 2
    first_width = 1
    extended = padded_2(background, (("gx", 1), ("gy", 2)), reach)
    first_ext = padded_2(adjoint[0], (("gx", 1), ("gy", 2)), first_width)
    viscosity = eddy(extended[:3])
    drag_cells = jnp.where(is_main, extended[3], 0.0)

    def advance(adjoint_ext, extent):
        margin = reach - (extent - 1)
        wind_here = crop_xy(extended[:3], margin)
        drag_here = crop_xy(drag_cells, margin)
        visc_here = crop_xy(viscosity, reach - 1 - extent)
        position = anchor + jnp.arange(-(extent - 1), cells_x + extent - 1, dtype=jnp.int32)
        fringe_rates = ramp(position, fringe_range, length_total)[:, None, None]
        centre, rate_term = tendency(adjoint_ext, wind_here, visc_here, drag_here)
        forcing = fringe_rates * centre[:3]
        incoming = passed_along(forcing, "dom", 1)
        own_part = jnp.where(is_main, forcing, 0.0)
        velocity = centre[:3] + DT * (rate_term[:3] - own_part + incoming)
        pressure = centre[3:] + DT * rate_term[3:]
        return jnp.concatenate([velocity, pressure], 0)

    current = advance(first_ext, first_width)
    current = advance(padded_2(current, (("gx", 1), ("gy", 2)), 1), 1)
    return current[None]


def solution(mesh):
    in_specs = (
        P("dom", None, "gx", "gy", None),
        P("dom", None, "gx", "gy", None),
        P("gx", "gy", None),
        P(),
    )
    out_specs = P("dom", None, "gx", "gy", None)
    return jax.shard_map(
        on_device, mesh=mesh, in_specs=in_specs, out_specs=out_specs, check_vma=False
    )
```

profile of v0, /device:TPU:198, one launch (start us, length us, event | category | flops | bytes accessed | tf_op | source)
XLA Modules:
  0.0 95.6 jit_solution(17155360830508600387)
XLA Ops:
  0.0 0.9 fusion.98
  0.9 10.9 %collective-permute-start.1 = (f32[4,1,16,128]{3,2,1,0:T(8,128)S(1)}, f32[4,1,16,128]{3,2,1,0:T(8,128)S(1)}, u32[]{:S(2)}, u32[]{:S(2)}) collective-permute-start(f32[4,1,16,128]{3,2,1,0:T(8,128)S(1)} %get-tuple-element.39), channel_id=1, source_target_pairs={{0,16},{16,32},{32,48},{48,64},{64,80},{80,96},{96,112},{112,128},... | collective-permute-start | bytes 98312 | tf_op jit(solution)/shard_map/ppermute | solution.py:22
  11.8 9.4 %collective-permute-start = (f32[4,1,16,128]{3,2,1,0:T(8,128)S(1)}, f32[4,1,16,128]{3,2,1,0:T(8,128)S(1)}, u32[]{:S(2)}, u32[]{:S(2)}) collective-permute-start(f32[4,1,16,128]{3,2,1,0:T(8,128)S(1)} %get-tuple-element.40), channel_id=1, source_target_pairs={{16,0},{32,16},{48,32},{64,48},{80,64},{96,80},{112,96},{128,112},... | collective-permute-start | bytes 98312 | tf_op jit(solution)/shard_map/ppermute | solution.py:23
  21.2 0.9 convert_bitcast_fusion
  22.1 0.8 pad_maximum_fusion.19
  23.0 1.9 %collective-permute-start.4 = (f32[4,2,16,128]{3,2,1,0:T(8,128)S(1)}, f32[4,2,16,128]{3,2,1,0:T(8,128)S(1)}, u32[]{:S(2)}, u32[]{:S(2)}) collective-permute-start(f32[4,2,16,128]{3,2,1,0:T(8,128)S(1)} %get-tuple-element.37), channel_id=1, source_target_pairs={{0,16},{16,32},{32,48},{48,64},{64,80},{80,96},{96,112},{112,128},... | collective-permute-start | bytes 196616 | tf_op jit(solution)/shard_map/ppermute | solution.py:22
  24.9 9.9 %collective-permute-start.5 = (f32[4,2,16,128]{3,2,1,0:T(8,128)S(1)}, f32[4,2,16,128]{3,2,1,0:T(8,128)S(1)}, u32[]{:S(2)}, u32[]{:S(2)}) collective-permute-start(f32[4,2,16,128]{3,2,1,0:T(8,128)S(1)} %get-tuple-element.38), channel_id=1, source_target_pairs={{16,0},{32,16},{48,32},{64,48},{80,64},{96,80},{112,96},{128,112},... | collective-permute-start | bytes 196616 | tf_op jit(solution)/shard_map/ppermute | solution.py:23
  34.8 1.3 %fusion.99 = (s32[1]{0:T(128)}, s32[1]{0:T(128)}) fusion(s32[2]{0:T(128)} %param.7), kind=kLoop, calls=%fused_computation.205 | loop fusion | bytes 16 | tf_op jit(solution)/shard_map/slice | solution.py:98
  36.8 1.3 %compare_select_fusion.2 = f32[16]{0:T(128)S(1)} fusion(f32[]{:T(128)S(6)} %convert_element_type.32, s32[]{:T(128)} %bitcast.16, s32[]{:T(128)} %bitcast.15, s32[]{:T(128)S(6)} %mul.435), kind=kLoop, calls=%fused_computation.198 | loop fusion | flops 336 | bytes 80 | tf_op jit(solution)/shard_map/jit(_where)/select_n | solution.py:102
  38.1 1.1 %broadcast_multiply_fusion.7 = f32[3,16,16,128]{3,2,1,0:T(8,128)S(1)} fusion(f32[16]{0:T(128)S(1)} %compare_select_fusion.2, f32[1,4,16,16,128]{4,3,2,1,0:T(8,128)} %param.5), kind=kLoop, calls=%fused_computation.153 | loop fusion | flops 98304 | bytes 786496 | tf_op jit(solution)/shard_map/mul | solution.py:126
  39.2 1.3 %collective-permute-start.8 = (f32[3,16,16,128]{3,2,1,0:T(8,128)S(1)}, f32[3,16,16,128]{3,2,1,0:T(8,128)S(1)}, u32[]{:S(2)}, u32[]{:S(2)}) collective-permute-start(f32[3,16,16,128]{3,2,1,0:T(8,128)S(1)} %broadcast_multiply_fusion.7), channel_id=1, source_target_pairs={{0,512},{1,513},{2,514},{3,515},{4,516},{5,517},{6,518},{7,519},{8... | collective-permute-start | bytes 1179656 | tf_op jit(solution)/shard_map/ppermute | solution.py:31
  40.6 0.0 collective-permute-done.1
  40.6 0.1 pad_maximum_fusion.24
  40.7 3.8 %collective-permute-start.3 = (f32[4,18,1,128]{3,2,1,0:T(1,128)S(1)}, f32[4,18,1,128]{3,2,1,0:T(1,128)S(1)}, u32[]{:S(2)}, u32[]{:S(2)}) collective-permute-start(f32[4,18,1,128]{3,2,1,0:T(1,128)S(1)} %get-tuple-element.23), channel_id=1, source_target_pairs={{0,1},{1,2},{2,3},{3,4},{4,5},{5,6},{6,7},{7,8},{8,9},{9,10},{10,1... | collective-permute-start | bytes 110600 | tf_op jit(solution)/shard_map/ppermute | solution.py:22
  44.5 2.0 %collective-permute-start.2 = (f32[4,18,1,128]{3,2,1,0:T(1,128)S(1)}, f32[4,18,1,128]{3,2,1,0:T(1,128)S(1)}, u32[]{:S(2)}, u32[]{:S(2)}) collective-permute-start(f32[4,18,1,128]{3,2,1,0:T(1,128)S(1)} %get-tuple-element.24), channel_id=1, source_target_pairs={{1,0},{2,1},{3,2},{4,3},{5,4},{6,5},{7,6},{8,7},{9,8},{10,9},{11,1... | collective-permute-start | bytes 110600 | tf_op jit(solution)/shard_map/ppermute | solution.py:23
  46.6 0.0 collective-permute-done.5
  46.6 0.1 pad_maximum_fusion.17
  46.7 7.7 %collective-permute-start.6 = (f32[4,20,2,128]{3,2,1,0:T(2,128)S(1)}, f32[4,20,2,128]{3,2,1,0:T(2,128)S(1)}, u32[]{:S(2)}, u32[]{:S(2)}) collective-permute-start(f32[4,20,2,128]{3,2,1,0:T(2,128)S(1)} %get-tuple-element.15), channel_id=1, source_target_pairs={{0,1},{1,2},{2,3},{3,4},{4,5},{5,6},{6,7},{7,8},{8,9},{9,10},{10,1... | collective-permute-start | bytes 245768 | tf_op jit(solution)/shard_map/ppermute | solution.py:22
  54.4 1.9 %collective-permute-start.7 = (f32[4,20,2,128]{3,2,1,0:T(2,128)S(1)}, f32[4,20,2,128]{3,2,1,0:T(2,128)S(1)}, u32[]{:S(2)}, u32[]{:S(2)}) collective-permute-start(f32[4,20,2,128]{3,2,1,0:T(2,128)S(1)} %get-tuple-element.16), channel_id=1, source_target_pairs={{1,0},{2,1},{3,2},{4,3},{5,4},{6,5},{7,6},{8,7},{9,8},{10,9},{11,1... | collective-permute-start | bytes 245768 | tf_op jit(solution)/shard_map/ppermute | solution.py:23
  56.3 0.8 select_maximum_fusion.5
  57.2 0.2 pad_maximum_fusion.1
  57.3 0.4 multiply_add_fusion.1
  57.8 0.1 fusion.97
  57.9 7.7 %collective-permute-done.7 = f32[4,20,2,128]{3,2,1,0:T(2,128)S(1)} collective-permute-done((f32[4,20,2,128]{3,2,1,0:T(2,128)S(1)}, f32[4,20,2,128]{3,2,1,0:T(2,128)S(1)}, u32[]{:S(2)}, u32[]{:S(2)}) %collective-permute-start.7) | collective-permute-done | bytes 81952 | tf_op jit(solution)/shard_map/ppermute | solution.py:23
  65.5 0.2 pad_maximum_fusion
  65.7 0.1 fusion.5
  65.9 0.5 fusion.2
  66.4 0.3 fusion.58
  66.6 0.1 fusion.92
  66.7 0.1 slice_multiply_fusion
  66.8 0.1 fusion.82
  66.9 0.5 broadcast_multiply_fusion.6
  67.5 1.9 %collective-permute-start.10 = (f32[4,1,16,128]{3,2,1,0:T(8,128)S(1)}, f32[4,1,16,128]{3,2,1,0:T(8,128)S(1)}, u32[]{:S(2)}, u32[]{:S(2)}) collective-permute-start(f32[4,1,16,128]{3,2,1,0:T(8,128)S(1)} %get-tuple-element.31), channel_id=1, source_target_pairs={{0,16},{16,32},{32,48},{48,64},{64,80},{80,96},{96,112},{112,128},... | collective-permute-start | bytes 98312 | tf_op jit(solution)/shard_map/ppermute | solution.py:22
  69.4 9.9 %collective-permute-start.9 = (f32[4,1,16,128]{3,2,1,0:T(8,128)S(1)}, f32[4,1,16,128]{3,2,1,0:T(8,128)S(1)}, u32[]{:S(2)}, u32[]{:S(2)}) collective-permute-start(f32[4,1,16,128]{3,2,1,0:T(8,128)S(1)} %get-tuple-element.32), channel_id=1, source_target_pairs={{16,0},{32,16},{48,32},{64,48},{80,64},{96,80},{112,96},{128,112},... | collective-permute-start | bytes 98312 | tf_op jit(solution)/shard_map/ppermute | solution.py:23
  79.4 1.3 %collective-permute-start.13 = (f32[3,16,16,128]{3,2,1,0:T(8,128)S(1)}, f32[3,16,16,128]{3,2,1,0:T(8,128)S(1)}, u32[]{:S(2)}, u32[]{:S(2)}) collective-permute-start(f32[3,16,16,128]{3,2,1,0:T(8,128)S(1)} %get-tuple-element.5), channel_id=1, source_target_pairs={{0,512},{1,513},{2,514},{3,515},{4,516},{5,517},{6,518},{7,519},{8... | collective-permute-start | bytes 1179656 | tf_op jit(solution)/shard_map/ppermute | solution.py:31
  80.7 0.0 collective-permute-done.10
  80.7 0.2 collective-permute-done.9
  81.0 0.1 pad_maximum_fusion.20
  81.0 1.9 %collective-permute-start.12 = (f32[4,18,1,128]{3,2,1,0:T(1,128)S(1)}, f32[4,18,1,128]{3,2,1,0:T(1,128)S(1)}, u32[]{:S(2)}, u32[]{:S(2)}) collective-permute-start(f32[4,18,1,128]{3,2,1,0:T(1,128)S(1)} %get-tuple-element.19), channel_id=1, source_target_pairs={{0,1},{1,2},{2,3},{3,4},{4,5},{5,6},{6,7},{7,8},{8,9},{9,10},{10,1... | collective-permute-start | bytes 110600 | tf_op jit(solution)/shard_map/ppermute | solution.py:22
  82.9 3.9 %collective-permute-start.11 = (f32[4,18,1,128]{3,2,1,0:T(1,128)S(1)}, f32[4,18,1,128]{3,2,1,0:T(1,128)S(1)}, u32[]{:S(2)}, u32[]{:S(2)}) collective-permute-start(f32[4,18,1,128]{3,2,1,0:T(1,128)S(1)} %get-tuple-element.20), channel_id=1, source_target_pairs={{1,0},{2,1},{3,2},{4,3},{5,4},{6,5},{7,6},{8,7},{9,8},{10,9},{11,1... | collective-permute-start | bytes 110600 | tf_op jit(solution)/shard_map/ppermute | solution.py:23
  86.9 0.1 pad_maximum_fusion.11
  87.0 5.7 %collective-permute-done.11 = f32[4,18,1,128]{3,2,1,0:T(1,128)S(1)} collective-permute-done((f32[4,18,1,128]{3,2,1,0:T(1,128)S(1)}, f32[4,18,1,128]{3,2,1,0:T(1,128)S(1)}, u32[]{:S(2)}, u32[]{:S(2)}) %collective-permute-start.11) | collective-permute-done | bytes 36896 | tf_op jit(solution)/shard_map/ppermute | solution.py:23
  92.7 0.8 select_maximum_fusion
  93.5 0.2 pad_maximum_fusion.2
  93.7 0.4 multiply_add_fusion
  94.1 0.1 fusion.96
  94.2 0.5 fusion.32
  94.7 0.8 maximum_bitcast_fusion
  (18 shorter events, 0.2 us)
Async XLA Ops:
  0.0 40.5 %copy-start = (f32[1,4,16,16,128]{4,3,2,1,0:T(8,128)S(1)}, f32[1,4,16,16,128]{4,3,2,1,0:T(8,128)}, u32[]{:S(2)}) copy-start(f32[1,4,16,16,128]{4,3,2,1,0:T(8,128)} %param.5) | copy-start | bytes 1572868
  0.0 40.6 %copy-start.1 = (f32[1,3,16,16,128]{4,3,2,1,0:T(8,128)S(1)}, f32[1,3,16,16,128]{4,3,2,1,0:T(8,128)}, u32[]{:S(2)}) copy-start(f32[1,3,16,16,128]{4,3,2,1,0:T(8,128)} %param.4) | copy-start | bytes 1179652
  0.9 39.8 %collective-permute-start.1 = (f32[4,1,16,128]{3,2,1,0:T(8,128)S(1)}, f32[4,1,16,128]{3,2,1,0:T(8,128)S(1)}, u32[]{:S(2)}, u32[]{:S(2)}) collective-permute-start(f32[4,1,16,128]{3,2,1,0:T(8,128)S(1)} %get-tuple-element.39), channel_id=1, source_target_pairs={{0,16},{16,32},{32,48},{48,64},{64,80},{80,96},{96,112},{112,128},... | collective-permute-start | bytes 98312 | tf_op jit(solution)/shard_map/ppermute | solution.py:22
  11.8 28.9 %collective-permute-start = (f32[4,1,16,128]{3,2,1,0:T(8,128)S(1)}, f32[4,1,16,128]{3,2,1,0:T(8,128)S(1)}, u32[]{:S(2)}, u32[]{:S(2)}) collective-permute-start(f32[4,1,16,128]{3,2,1,0:T(8,128)S(1)} %get-tuple-element.40), channel_id=1, source_target_pairs={{16,0},{32,16},{48,32},{64,48},{80,64},{96,80},{112,96},{128,112},... | collective-permute-start | bytes 98312 | tf_op jit(solution)/shard_map/ppermute | solution.py:23
  23.0 23.6 %collective-permute-start.4 = (f32[4,2,16,128]{3,2,1,0:T(8,128)S(1)}, f32[4,2,16,128]{3,2,1,0:T(8,128)S(1)}, u32[]{:S(2)}, u32[]{:S(2)}) collective-permute-start(f32[4,2,16,128]{3,2,1,0:T(8,128)S(1)} %get-tuple-element.37), channel_id=1, source_target_pairs={{0,16},{16,32},{32,48},{48,64},{64,80},{80,96},{96,112},{112,128},... | collective-permute-start | bytes 196616 | tf_op jit(solution)/shard_map/ppermute | solution.py:22
  24.9 21.7 %collective-permute-start.5 = (f32[4,2,16,128]{3,2,1,0:T(8,128)S(1)}, f32[4,2,16,128]{3,2,1,0:T(8,128)S(1)}, u32[]{:S(2)}, u32[]{:S(2)}) collective-permute-start(f32[4,2,16,128]{3,2,1,0:T(8,128)S(1)} %get-tuple-element.38), channel_id=1, source_target_pairs={{16,0},{32,16},{48,32},{64,48},{80,64},{96,80},{112,96},{128,112},... | collective-permute-start | bytes 196616 | tf_op jit(solution)/shard_map/ppermute | solution.py:23
  39.2 27.7 %collective-permute-start.8 = (f32[3,16,16,128]{3,2,1,0:T(8,128)S(1)}, f32[3,16,16,128]{3,2,1,0:T(8,128)S(1)}, u32[]{:S(2)}, u32[]{:S(2)}) collective-permute-start(f32[3,16,16,128]{3,2,1,0:T(8,128)S(1)} %broadcast_multiply_fusion.7), channel_id=1, source_target_pairs={{0,512},{1,513},{2,514},{3,515},{4,516},{5,517},{6,518},{7,519},{8... | collective-permute-start | bytes 1179656 | tf_op jit(solution)/shard_map/ppermute | solution.py:31
  40.7 15.6 %collective-permute-start.3 = (f32[4,18,1,128]{3,2,1,0:T(1,128)S(1)}, f32[4,18,1,128]{3,2,1,0:T(1,128)S(1)}, u32[]{:S(2)}, u32[]{:S(2)}) collective-permute-start(f32[4,18,1,128]{3,2,1,0:T(1,128)S(1)} %get-tuple-element.23), channel_id=1, source_target_pairs={{0,1},{1,2},{2,3},{3,4},{4,5},{5,6},{6,7},{7,8},{8,9},{9,10},{10,1... | collective-permute-start | bytes 110600 | tf_op jit(solution)/shard_map/ppermute | solution.py:22
  44.5 11.8 %collective-permute-start.2 = (f32[4,18,1,128]{3,2,1,0:T(1,128)S(1)}, f32[4,18,1,128]{3,2,1,0:T(1,128)S(1)}, u32[]{:S(2)}, u32[]{:S(2)}) collective-permute-start(f32[4,18,1,128]{3,2,1,0:T(1,128)S(1)} %get-tuple-element.24), channel_id=1, source_target_pairs={{1,0},{2,1},{3,2},{4,3},{5,4},{6,5},{7,6},{8,7},{9,8},{10,9},{11,1... | collective-permute-start | bytes 110600 | tf_op jit(solution)/shard_map/ppermute | solution.py:23
  46.7 11.2 %collective-permute-start.6 = (f32[4,20,2,128]{3,2,1,0:T(2,128)S(1)}, f32[4,20,2,128]{3,2,1,0:T(2,128)S(1)}, u32[]{:S(2)}, u32[]{:S(2)}) collective-permute-start(f32[4,20,2,128]{3,2,1,0:T(2,128)S(1)} %get-tuple-element.15), channel_id=1, source_target_pairs={{0,1},{1,2},{2,3},{3,4},{4,5},{5,6},{6,7},{7,8},{8,9},{9,10},{10,1... | collective-permute-start | bytes 245768 | tf_op jit(solution)/shard_map/ppermute | solution.py:22
  54.4 11.2 %collective-permute-start.7 = (f32[4,20,2,128]{3,2,1,0:T(2,128)S(1)}, f32[4,20,2,128]{3,2,1,0:T(2,128)S(1)}, u32[]{:S(2)}, u32[]{:S(2)}) collective-permute-start(f32[4,20,2,128]{3,2,1,0:T(2,128)S(1)} %get-tuple-element.16), channel_id=1, source_target_pairs={{1,0},{2,1},{3,2},{4,3},{5,4},{6,5},{7,6},{8,7},{9,8},{10,9},{11,1... | collective-permute-start | bytes 245768 | tf_op jit(solution)/shard_map/ppermute | solution.py:23
  67.5 13.2 %collective-permute-start.10 = (f32[4,1,16,128]{3,2,1,0:T(8,128)S(1)}, f32[4,1,16,128]{3,2,1,0:T(8,128)S(1)}, u32[]{:S(2)}, u32[]{:S(2)}) collective-permute-start(f32[4,1,16,128]{3,2,1,0:T(8,128)S(1)} %get-tuple-element.31), channel_id=1, source_target_pairs={{0,16},{16,32},{32,48},{48,64},{64,80},{80,96},{96,112},{112,128},... | collective-permute-start | bytes 98312 | tf_op jit(solution)/shard_map/ppermute | solution.py:22
  69.4 11.5 %collective-permute-start.9 = (f32[4,1,16,128]{3,2,1,0:T(8,128)S(1)}, f32[4,1,16,128]{3,2,1,0:T(8,128)S(1)}, u32[]{:S(2)}, u32[]{:S(2)}) collective-permute-start(f32[4,1,16,128]{3,2,1,0:T(8,128)S(1)} %get-tuple-element.32), channel_id=1, source_target_pairs={{16,0},{32,16},{48,32},{64,48},{80,64},{96,80},{112,96},{128,112},... | collective-permute-start | bytes 98312 | tf_op jit(solution)/shard_map/ppermute | solution.py:23
  79.4 14.8 %collective-permute-start.13 = (f32[3,16,16,128]{3,2,1,0:T(8,128)S(1)}, f32[3,16,16,128]{3,2,1,0:T(8,128)S(1)}, u32[]{:S(2)}, u32[]{:S(2)}) collective-permute-start(f32[3,16,16,128]{3,2,1,0:T(8,128)S(1)} %get-tuple-element.5), channel_id=1, source_target_pairs={{0,512},{1,513},{2,514},{3,515},{4,516},{5,517},{6,518},{7,519},{8... | collective-permute-start | bytes 1179656 | tf_op jit(solution)/shard_map/ppermute | solution.py:31
  81.0 6.0 %collective-permute-start.12 = (f32[4,18,1,128]{3,2,1,0:T(1,128)S(1)}, f32[4,18,1,128]{3,2,1,0:T(1,128)S(1)}, u32[]{:S(2)}, u32[]{:S(2)}) collective-permute-start(f32[4,18,1,128]{3,2,1,0:T(1,128)S(1)} %get-tuple-element.19), channel_id=1, source_target_pairs={{0,1},{1,2},{2,3},{3,4},{4,5},{5,6},{6,7},{7,8},{8,9},{9,10},{10,1... | collective-permute-start | bytes 110600 | tf_op jit(solution)/shard_map/ppermute | solution.py:22
  82.9 9.8 %collective-permute-start.11 = (f32[4,18,1,128]{3,2,1,0:T(1,128)S(1)}, f32[4,18,1,128]{3,2,1,0:T(1,128)S(1)}, u32[]{:S(2)}, u32[]{:S(2)}) collective-permute-start(f32[4,18,1,128]{3,2,1,0:T(1,128)S(1)} %get-tuple-element.20), channel_id=1, source_target_pairs={{1,0},{2,1},{3,2},{4,3},{5,4},{6,5},{7,6},{8,7},{9,8},{10,9},{11,1... | collective-permute-start | bytes 110600 | tf_op jit(solution)/shard_map/ppermute | solution.py:23
where the time goes:
time: 96.2 us; the launch traced here: 95.6 us
  starting transfers between devices  68 us (71%)
  waiting for transfers between devices  13.7 us (14%)
  other arithmetic  10.6 us (11%)
  local copies, waits for them, and re-layouts  2.29 us (2%)
  between operations  1.03 us (1%)
    ppermute x6, starting transfers between devices, padded_2(): after = lax.ppermute(leading, axis, down)  37.2 us
    ppermute x6, starting transfers between devices, padded_2(): before = lax.ppermute(last, axis, up)  28.2 us
    ppermute x6, waiting for transfers between devices, padded_2(): after = lax.ppermute(leading, axis, down)  13.6 us
    ppermute x2, starting transfers between devices, passed_along(): return lax.ppermute(shard, axis, pairs)  2.63 us
    concatenate x8, other arithmetic, padded_2(): shard = jnp.concatenate([before, shard, after], axis=dim)  2.34 us
  transfers between devices with their start and end apart: 14, of which 3 were waited for; matrix products, arithmetic and copies ran while one was open for 11% of the time, Pallas kernels for 0%

commit v1 on v0

v1 whole, which is shorter than its diff:
```python
import functools
import math

import jax
import jax.numpy as jnp
from jax import lax
from jax.experimental import pallas as pl
from jax.experimental.pallas import tpu as pltpu
from jax.sharding import PartitionSpec as P

DT = 0.1
SMAG = 0.1
SOUND_SQ = 4.0
DRAG = 1.0
RATE = 3.0

T = 16
NZ = 128
R = 24
F32 = jnp.float32
VMEM = pl.BlockSpec(memory_space=pltpu.VMEM)
SMEM = pl.BlockSpec(memory_space=pltpu.SMEM)

Y_WIND, Y_ADJ, Y_DRAG, Y_LEN = 0, 9, 17, 18
X_U1, X_U2, X_A1, X_A2, X_NU2, X_D1, X_LEN = 0, 60, 114, 186, 250, 266, 288


def shape(*dims):
    return jax.ShapeDtypeStruct(dims, F32)


def call(body, outs, n_in, scratch=(), specs=None):
    return pl.pallas_call(
        body,
        out_shape=outs,
        in_specs=[VMEM] * n_in if specs is None else specs,
        out_specs=jax.tree.map(lambda _: VMEM, outs),
        scratch_shapes=[pltpu.VMEM(s, F32) for s in scratch],
    )


def is_main():
    return (lax.axis_index("dom") == 0).astype(F32)


def up_z(v):
    return pltpu.roll(v, NZ - 1, 1)


def down_z(v):
    return pltpu.roll(v, 1, 1)


def edges_z(rows):
    lane = lax.broadcasted_iota(jnp.int32, (rows, NZ), 1)
    return (lane < NZ - 1).astype(F32), (lane > 0).astype(F32)


def drag_rows(u, v, w, turb):
    return (DT * DRAG) * turb * jnp.sqrt(u * u + v * v + w * w) * is_main()


def pack_y(w, a, t, up, dn):
    for msg, edge in ((up, T - 3), (dn, 0)):
        near = 0 if edge == 0 else T - 1
        for c in range(3):
            for l in range(3):
                msg[Y_WIND + 3 * c + l] = w[c, pl.ds(edge + l, T, stride=T), :]
        for c in range(4):
            for l in range(2):
                at = l if edge == 0 else T - 2 + l
                msg[Y_ADJ + 2 * c + l] = a[c, pl.ds(at, T, stride=T), :]
        u, v, z = (w[c, pl.ds(near, T, stride=T), :] for c in range(3))
        turb = t[pl.ds(near, T, stride=T), :].astype(F32)
        msg[Y_DRAG] = drag_rows(u, v, z, turb)


def nu_row(ew, base, at, ones_p, ones_m, rows=R):
    g = []
    for c in range(3):
        mid = ew[c, pl.ds(at, rows), :]
        gx = ew[c, pl.ds(at + R, rows), :] - ew[c, pl.ds(at - R, rows), :]
        gy = ew[c, pl.ds(at + 1, rows), :] - ew[c, pl.ds(at - 1, rows), :]
        gz = up_z(mid) * ones_p - down_z(mid) * ones_m
        g.append((gx, gy, gz))
    diag = g[0][0] * g[0][0] + g[1][1] * g[1][1] + g[2][2] * g[2][2]
    xy = g[1][0] + g[0][1]
    xz = g[2][0] + g[0][2]
    yz = g[2][1] + g[1][2]
    return SMAG * jnp.sqrt(0.5 * diag + 0.25 * (xy * xy + xz * xz + yz * yz))


def pack_x(w, a, t, lo, hi, up, dn, ew, ea, ed):
    for c in range(3):
        for x in range(T):
            ew[c, pl.ds(x * R + 3, T), :] = w[c, pl.ds(x * T, T), :]
        for l in range(3):
            ew[c, pl.ds(l, T, stride=R), :] = lo[Y_WIND + 3 * c + l]
            ew[c, pl.ds(T + 3 + l, T, stride=R), :] = hi[Y_WIND + 3 * c + l]
    for c in range(4):
        for x in range(T):
            ea[c, pl.ds(x * R + 3, T), :] = a[c, pl.ds(x * T, T), :]
        for l in range(2):
            ea[c, pl.ds(1 + l, T, stride=R), :] = lo[Y_ADJ + 2 * c + l]
            ea[c, pl.ds(T + 3 + l, T, stride=R), :] = hi[Y_ADJ + 2 * c + l]
    main = is_main()
    for x in range(T):
        u, v, z = (w[c, pl.ds(x * T, T), :] for c in range(3))
        turb = t[pl.ds(x * T, T), :].astype(F32)
        ed[pl.ds(x * R + 3, T), :] = drag_rows(u, v, z, turb)
    ed[pl.ds(2, T, stride=R), :] = lo[Y_DRAG]
    ed[pl.ds(T + 3, T, stride=R), :] = hi[Y_DRAG]
    ones_p, ones_m = edges_z(T)
    for msg, x1, x2 in ((up, T - 1, T - 2), (dn, 0, 1)):
        for c in range(3):
            msg[pl.ds(X_U1 + 20 * c, 20), :] = ew[c, pl.ds(x1 * R + 1, 20), :]
            msg[pl.ds(X_U2 + 18 * c, 18), :] = ew[c, pl.ds(x2 * R + 2, 18), :]
        for c in range(4):
            msg[pl.ds(X_A1 + 18 * c, 18), :] = ea[c, pl.ds(x1 * R + 2, 18), :]
            msg[pl.ds(X_A2 + 16 * c, 16), :] = ea[c, pl.ds(x2 * R + 3, 16), :]
        msg[pl.ds(X_NU2, 16), :] = nu_row(ew, 0, x2 * R + 3, ones_p, ones_m, 16)
        msg[pl.ds(X_D1, 16), :] = ed[pl.ds(x1 * R + 3, 16), :]
        msg[pl.ds(X_D1 + 16, 6), :] = jnp.zeros((6, NZ), F32)


def fringe_table(fringe, table, rows):
    total = T * lax.axis_size("gx")
    x = lax.broadcasted_iota(jnp.int32, (rows, NZ), 0) - 1
    place = lax.axis_index("gx") * T + x - fringe[0]
    offset = lax.rem(place + 2 * total, jnp.full_like(place, total))
    width = fringe[1]
    phase = (math.pi * (offset.astype(F32) + 0.5)) / jnp.full((rows, NZ), width, jnp.int32).astype(F32)
    sine = jnp.sin(phase)
    table[...] = jnp.where(offset < width, (DT * RATE) * (sine * sine), 0.0)


def stencil(a, at, step, rows, coefs, wind, ones_p, ones_m):
    c0, cxp, cxm, cyp, cym, czp, czm = coefs
    new, dx, dy, dz = [], [], [], []
    for c in range(4):
        mid = a[c, pl.ds(at, rows), :]
        xp, xm = a[c, pl.ds(at + step, rows), :], a[c, pl.ds(at - step, rows), :]
        yp, ym = a[c, pl.ds(at + 1, rows), :], a[c, pl.ds(at - 1, rows), :]
        zp, zm = up_z(mid), down_z(mid)
        if c < 3:
            new.append(c0 * mid + (cxp * xp + cxm * xm) + (cyp * yp + cym * ym) + (czp * zp + czm * zm))
        else:
            new.append(mid)
        dx.append(xp - xm)
        dy.append(yp - ym)
        dz.append(zp * ones_p - zm * ones_m)
    half = 0.5 * DT
    sound = half * SOUND_SQ
    new[0] = new[0] + sound * dx[3]
    new[1] = new[1] + sound * dy[3]
    new[2] = new[2] + sound * dz[3]
    u, v, w = wind
    new[3] = new[3] + half * (u * dx[3] + v * dy[3] + w * dz[3] + dx[0] + dy[1] + dz[2])
    return new


def first_step(w, a, d, lo, hi, main_a, fringe, a1, cf, sent, ew, ea, ed, nu, table):
    main = is_main()
    fringe_table(fringe, table, R)
    for c in range(3):
        ew[c, pl.ds(2 * R, T * R), :] = w[c]
    for c in range(4):
        ea[c, pl.ds(2 * R, T * R), :] = a[c]
    ed[pl.ds(R, T * R), :] = d[...]
    for msg, p1, p2 in ((lo, 1, 0), (hi, T + 2, T + 3)):
        for c in range(3):
            ew[c, pl.ds(p1 * R + 1, 20), :] = msg[pl.ds(X_U1 + 20 * c, 20), :]
            ew[c, pl.ds(p2 * R + 2, 18), :] = msg[pl.ds(X_U2 + 18 * c, 18), :]
        for c in range(4):
            ea[c, pl.ds(p1 * R + 2, 18), :] = msg[pl.ds(X_A1 + 18 * c, 18), :]
            ea[c, pl.ds(p2 * R + 3, 16), :] = msg[pl.ds(X_A2 + 16 * c, 16), :]
        nu[pl.ds(p2 * R + 3, 16), :] = (0.5 * DT) * msg[pl.ds(X_NU2, 16), :]
        ed[pl.ds((p1 - 1) * R + 3, 16), :] = msg[pl.ds(X_D1, 16), :]
    ones_p, ones_m = edges_z(R)

    def nu_plane(x, _):
        at = pl.multiple_of(x * R, 8)
        nu[pl.ds(at, R), :] = (0.5 * DT) * nu_row(ew, 0, at, ones_p, ones_m)
        return 0

    lax.fori_loop(1, T + 3, nu_plane, 0)

    def plane(x, _):
        at = pl.multiple_of((x + 1) * R, 8)
        out = pl.multiple_of(x * R, 8)
        wind = [ew[c, pl.ds(at, R), :] for c in range(3)]
        h = nu[pl.ds(at, R), :]
        hxp, hxm = nu[pl.ds(at + R, R), :], nu[pl.ds(at - R, R), :]
        hyp, hym = nu[pl.ds(at + 1, R), :], nu[pl.ds(at - 1, R), :]
        hzp, hzm = up_z(h) * ones_p, down_z(h) * ones_m
        rate = jnp.broadcast_to(table[pl.ds(x, 1), :], (R, NZ))
        half = 0.5 * DT
        lost = ed[pl.ds(out, R), :] + main * rate
        c0 = (1.0 - lost) - (6.0 * h + (hxp + hxm) + (hyp + hym) + (hzp + hzm))
        pu, pv, pw = (half * v for v in wind)
        coefs = (
            c0,
            h + hxp + pu,
            h + hxm - pu,
            h + hyp + pv,
            h + hym - pv,
            (h + hzp + pw) * ones_p,
            (h + hzm - pw) * ones_m,
        )
        new = stencil(ea, at, R, R, coefs, wind, ones_p, ones_m)
        for c in range(4):
            a1[c, pl.ds(out, R), :] = new[c]
        for k in range(7):
            cf[k, pl.ds(out, R), :] = coefs[k]
        return 0

    lax.fori_loop(0, T + 2, plane, 0)
    for c in range(3):
        for x, p in ((0, 1), (T + 1, T + 2)):
            sent[c, pl.ds(x * T, T), :] = ea[c, pl.ds(p * R + 3, T), :]

    def force(x, _):
        out = pl.multiple_of((x + 1) * R, 8)
        src = pl.multiple_of(x * R, 8)
        rate = jnp.broadcast_to(table[pl.ds(x + 1, 1), :], (R, NZ)) * (1.0 - main)
        for c in range(3):
            v = a1[c, pl.ds(out, R), :] + rate * main_a[c, pl.ds(src, R), :]
            a1[c, pl.ds(out, R), :] = v
        for c in range(3):
            sent[c, pl.ds(pl.multiple_of((x + 1) * T, 8), T), :] = a1[c, pl.ds(out + 3, T), :]
        return 0

    lax.fori_loop(0, T, force, 0)


def second_step(w, a1, cf, main_a, fringe, out, table):
    other = 1.0 - is_main()
    fringe_table(fringe, table, R)
    ones_p, ones_m = edges_z(T)

    def plane(x, _):
        at = (x + 1) * R + 3
        own = pl.multiple_of(x * T, 8)
        wind = [w[c, pl.ds(own, T), :] for c in range(3)]
        coefs = [cf[k, pl.ds(at, T), :] for k in range(7)]
        new = stencil(a1, at, R, T, coefs, wind, ones_p, ones_m)
        rate = jnp.broadcast_to(table[pl.ds(x + 1, 1), :], (T, NZ)) * other
        for c in range(3):
            new[c] = new[c] + rate * main_a[c, pl.ds(pl.multiple_of((x + 1) * T, 8), T), :]
        for c in range(4):
            out[c, pl.ds(own, T), :] = new[c]
        return 0

    lax.fori_loop(0, T, plane, 0)
    for x, p, k, sign in ((0, 0, 2, -1.0), (T - 1, T + 1, 1, 1.0)):
        rate = jnp.broadcast_to(table[pl.ds(p, 1), :], (T, NZ)) * other
        beside = [rate * main_a[c, pl.ds(p * T, T), :] for c in range(3)]
        coef = cf[k, pl.ds((x + 1) * R + 3, T), :]
        for c in range(3):
            out[c, pl.ds(x * T, T), :] = out[c, pl.ds(x * T, T), :] + coef * beside[c]
        out[3, pl.ds(x * T, T), :] = out[3, pl.ds(x * T, T), :] + (sign * 0.5 * DT) * beside[0]


def ring(axis, by):
    devices = lax.axis_size(axis)
    return [(i, (i + by) % devices) for i in range(devices)]


def on_device(wind, adjoint, turbines, fringe_range):
    w = wind.reshape(3, T * T, NZ)
    a = adjoint.reshape(4, T * T, NZ)
    t = turbines.reshape(T * T, NZ)
    y_msg = shape(Y_LEN, T, NZ)
    up, dn = call(pack_y, (y_msg, y_msg), 3)(w, a, t)
    lo = lax.ppermute(up, "gy", ring("gy", 1))
    hi = lax.ppermute(dn, "gy", ring("gy", -1))
    x_msg = shape(X_LEN, NZ)
    up, dn, ew, ea, ed = call(
        pack_x, (x_msg, x_msg, shape(3, T * R, NZ), shape(4, T * R, NZ), shape(T * R, NZ)), 5
    )(w, a, t, lo, hi)
    xlo = lax.ppermute(up, "gx", ring("gx", 1))
    xhi = lax.ppermute(dn, "gx", ring("gx", -1))
    main_a = lax.ppermute(ea, "dom", [(0, 1)])
    a1, cf, sent = call(
        first_step,
        (shape(4, (T + 2) * R, NZ), shape(7, (T + 2) * R, NZ), shape(3, (T + 2) * T, NZ)),
        7,
        scratch=(
            (3, (T + 4) * R, NZ),
            (4, (T + 4) * R, NZ),
            ((T + 2) * R, NZ),
            ((T + 4) * R, NZ),
            (R, NZ),
        ),
        specs=[VMEM] * 6 + [SMEM],
    )(ew, ea, ed, xlo, xhi, main_a, fringe_range)
    main_a1 = lax.ppermute(sent, "dom", [(0, 1)])
    out = call(second_step, shape(4, T * T, NZ), 5, scratch=((R, NZ),), specs=[VMEM] * 4 + [SMEM])(
        w, a1, cf, main_a1, fringe_range
    )
    return out.reshape(1, 4, T, T, NZ)


def solution(mesh):
    in_specs = (
        P("dom", None, "gx", "gy", None),
        P("dom", None, "gx", "gy", None),
        P("gx", "gy", None),
        P(),
    )
    out_specs = P("dom", None, "gx", "gy", None)
    return jax.shard_map(
        on_device, mesh=mesh, in_specs=in_specs, out_specs=out_specs, check_vma=False
    )
```

time: 96.2 us -> 71.1 us (0.74)
  the two profiles are of different devices: /device:TPU:198 before, /device:TPU:1 now
where the time goes in v1:
time: 71.1 us; the launch traced here: 70.7 us
  starting transfers between devices  35.4 us (50%)
  waiting for transfers between devices  16.6 us (23%)
  Pallas kernels  16.2 us (23%)
  local copies, waits for them, and re-layouts  2.37 us (3%)
    ppermute x1, starting transfers between devices, on_device(): xlo = lax.ppermute(up, 'gx', ring('gx', 1))  11.1 us
    ppermute x1, waiting for transfers between devices, on_device(): xhi = lax.ppermute(dn, 'gx', ring('gx', -1))  10.7 us
    ppermute x1, starting transfers between devices, on_device(): xhi = lax.ppermute(dn, 'gx', ring('gx', -1))  9.28 us
    ppermute x1, starting transfers between devices, on_device(): hi = lax.ppermute(dn, 'gy', ring('gy', -1))  8.61 us
    pallas_call x1, Pallas kernels, on_device(): call(first_step, (shape(4, (T + 2) * R, NZ), shape(7, (T + 2) * R, NZ), s...  7.4 us
    pallas_call x1, Pallas kernels, on_device(): call(second_step, shape(4, T * T, NZ), 5, scratch=((R, NZ),), specs=[VMEM...  4.23 us
    ppermute x1, starting transfers between devices, on_device(): lo = lax.ppermute(up, 'gy', ring('gy', 1))  3.92 us
    pallas_call x1, Pallas kernels, on_device(): call(pack_x, (x_msg, x_msg, shape(3, T * R, NZ), shape(4, T * R, NZ), sha...  2.64 us
  transfers between devices with their start and end apart: 6, of which 5 were waited for; matrix products, arithmetic and copies ran while one was open for 0% of the time, Pallas kernels for 0%

profile of v1, /device:TPU:1, one launch (start us, length us, event | category | flops | bytes accessed | tf_op | source)
XLA Modules:
  0.0 70.7 jit_solution(17317927643066864023)
XLA Ops:
  0.0 1.9 %shard_map.46 = (f32[18,16,128]{2,1,0:T(8,128)}, f32[18,16,128]{2,1,0:T(8,128)}) custom-call(f32[3,256,128]{2,1,0:T(8,128)} %bitcast.4, f32[4,256,128]{2,1,0:T(8,128)} %bitcast.7, s32[256,128]{1,0:T(8,128)} %bitcast.9), custom_call_target="tpu_custom_call" | custom-call | tf_op jit(solution)/shard_map/pallas_call | solution.py:274
  1.9 3.9 %collective-permute-start = (f32[18,16,128]{2,1,0:T(8,128)}, f32[18,16,128]{2,1,0:T(8,128)S(1)}, u32[]{:S(2)}, u32[]{:S(2)}) collective-permute-start(f32[18,16,128]{2,1,0:T(8,128)} %get-tuple-element.15), channel_id=1, source_target_pairs={{0,1},{1,2},{2,3},{3,4},{4,5},{5,6},{6,7},{7,8},{8,9},{9,10},{10,1... | collective-permute-start | bytes 442376 | tf_op jit(solution)/shard_map/ppermute | solution.py:275
  5.9 8.6 %collective-permute-start.1 = (f32[18,16,128]{2,1,0:T(8,128)}, f32[18,16,128]{2,1,0:T(8,128)S(1)}, u32[]{:S(2)}, u32[]{:S(2)}) collective-permute-start(f32[18,16,128]{2,1,0:T(8,128)} %get-tuple-element.16), channel_id=1, source_target_pairs={{0,15},{1,0},{2,1},{3,2},{4,3},{5,4},{6,5},{7,6},{8,7},{9,8},{10,9... | collective-permute-start | bytes 442376 | tf_op jit(solution)/shard_map/ppermute | solution.py:276
  14.5 0.8 %collective-permute-done.lo = f32[18,16,128]{2,1,0:T(8,128)S(1)} collective-permute-done((f32[18,16,128]{2,1,0:T(8,128)}, f32[18,16,128]{2,1,0:T(8,128)S(1)}, u32[]{:S(2)}, u32[]{:S(2)}) %collective-permute-start) | collective-permute-done | bytes 147488 | tf_op jit(solution)/shard_map/ppermute | solution.py:275
  15.3 0.0 copy-start.4
  15.3 1.6 %collective-permute-done.1.hi = f32[18,16,128]{2,1,0:T(8,128)S(1)} collective-permute-done((f32[18,16,128]{2,1,0:T(8,128)}, f32[18,16,128]{2,1,0:T(8,128)S(1)}, u32[]{:S(2)}, u32[]{:S(2)}) %collective-permute-start.1) | collective-permute-done | bytes 147488 | tf_op jit(solution)/shard_map/ppermute | solution.py:276
  16.9 0.0 copy-done.4
  16.9 0.0 copy-start.5
  16.9 0.6 copy-done.5
  17.5 2.6 %shard_map.47 = (f32[288,128]{1,0:T(8,128)}, f32[288,128]{1,0:T(8,128)}, f32[3,384,128]{2,1,0:T(8,128)}, f32[4,384,128]{2,1,0:T(8,128)}, f32[384,128]{1,0:T(8,128)}) custom-call(f32[3,256,128]{2,1,0:T(8,128)} %bitcast.5, f32[4,256,128]{2,1,0:T(8,128)} %bitcast.8, s32[256,128]{1,0:T(8,128)} %bitcast.10, f32[18,16,128]{2,1,0:T(8,128)} %copy-done.4, ...), custom_call_target="tpu_custom_call" | custom-call | tf_op jit(solution)/shard_map/pallas_call | solution.py:278
  20.2 1.3 %collective-permute-start.4 = (f32[4,384,128]{2,1,0:T(8,128)}, f32[4,384,128]{2,1,0:T(8,128)S(1)}, u32[]{:S(2)}, u32[]{:S(2)}) collective-permute-start(f32[4,384,128]{2,1,0:T(8,128)} %get-tuple-element.18.a), channel_id=1, source_target_pairs={{0,512},{1,513},{2,514},{3,515},{4,516},{5,517},{6,518},{7,519},{8... | collective-permute-start | bytes 2359304 | tf_op jit(solution)/shard_map/ppermute | solution.py:283
  21.5 11.1 %collective-permute-start.2 = (f32[288,128]{1,0:T(8,128)}, f32[288,128]{1,0:T(8,128)S(1)}, u32[]{:S(2)}, u32[]{:S(2)}) collective-permute-start(f32[288,128]{1,0:T(8,128)} %get-tuple-element.20), channel_id=1, source_target_pairs={{0,16},{16,32},{32,48},{48,64},{64,80},{80,96},{96,112},{112,128},... | collective-permute-start | bytes 442376 | tf_op jit(solution)/shard_map/ppermute | solution.py:281
  32.6 9.3 %collective-permute-start.3 = (f32[288,128]{1,0:T(8,128)}, f32[288,128]{1,0:T(8,128)S(1)}, u32[]{:S(2)}, u32[]{:S(2)}) collective-permute-start(f32[288,128]{1,0:T(8,128)} %get-tuple-element.21), channel_id=1, source_target_pairs={{0,496},{16,0},{32,16},{48,32},{64,48},{80,64},{96,80},{112,96},{1... | collective-permute-start | bytes 442376 | tf_op jit(solution)/shard_map/ppermute | solution.py:282
  41.8 1.0 %collective-permute-done.2.lo = f32[288,128]{1,0:T(8,128)S(1)} collective-permute-done((f32[288,128]{1,0:T(8,128)}, f32[288,128]{1,0:T(8,128)S(1)}, u32[]{:S(2)}, u32[]{:S(2)}) %collective-permute-start.2) | collective-permute-done | bytes 147488 | tf_op jit(solution)/shard_map/ppermute | solution.py:281
  42.8 0.0 copy-start.2
  42.8 10.7 %collective-permute-done.3.hi = f32[288,128]{1,0:T(8,128)S(1)} collective-permute-done((f32[288,128]{1,0:T(8,128)}, f32[288,128]{1,0:T(8,128)S(1)}, u32[]{:S(2)}, u32[]{:S(2)}) %collective-permute-start.3) | collective-permute-done | bytes 147488 | tf_op jit(solution)/shard_map/ppermute | solution.py:282
  53.5 0.0 copy-start.3
  53.5 0.0 collective-permute-done.4.main_a
  53.5 0.0 copy-start
  53.5 0.0 copy-done.2
  53.5 0.7 copy-done.3
  54.1 0.3 copy-done
  54.4 7.4 %shard_map.48 = (f32[4,432,128]{2,1,0:T(8,128)}, f32[7,432,128]{2,1,0:T(8,128)}, f32[3,288,128]{2,1,0:T(8,128)}) custom-call(f32[3,384,128]{2,1,0:T(8,128)} %get-tuple-element.17.w, f32[4,384,128]{2,1,0:T(8,128)} %get-tuple-element.18.a, f32[384,128]{1,0:T(8,128)} %get-tuple-element.19.d, f32[288,128]{1,0:T(8,128)} %copy-done.2, f32[288,128]{1,0:T(8,128)} %copy-done.3, ...), custom_call_target="tpu_custom_call" | custom-call | tf_op jit(solution)/shard_map/pallas_call | solution.py:284
  61.8 1.3 %collective-permute-start.5 = (f32[3,288,128]{2,1,0:T(8,128)}, f32[3,288,128]{2,1,0:T(8,128)S(1)}, u32[]{:S(2)}, u32[]{:S(2)}) collective-permute-start(f32[3,288,128]{2,1,0:T(8,128)} %get-tuple-element.24), channel_id=1, source_target_pairs={{0,512},{1,513},{2,514},{3,515},{4,516},{5,517},{6,518},{7,519},{8... | collective-permute-start | bytes 1327112 | tf_op jit(solution)/shard_map/ppermute | solution.py:297
  63.1 2.6 %collective-permute-done.5.main_a = f32[3,288,128]{2,1,0:T(8,128)S(1)} collective-permute-done((f32[3,288,128]{2,1,0:T(8,128)}, f32[3,288,128]{2,1,0:T(8,128)S(1)}, u32[]{:S(2)}, u32[]{:S(2)}) %collective-permute-start.5) | collective-permute-done | bytes 442400 | tf_op jit(solution)/shard_map/ppermute | solution.py:297
  65.7 0.0 copy-start.1
  65.7 0.8 %copy-done.1 = f32[3,288,128]{2,1,0:T(8,128)} copy-done((f32[3,288,128]{2,1,0:T(8,128)}, f32[3,288,128]{2,1,0:T(8,128)S(1)}, u32[]{:S(2)}) %copy-start.1) | copy-done | bytes 442392
  66.5 4.2 %shard_map.49 = f32[4,256,128]{2,1,0:T(8,128)} custom-call(f32[3,256,128]{2,1,0:T(8,128)} %bitcast.6, f32[4,432,128]{2,1,0:T(8,128)} %get-tuple-element.22.a1, f32[7,432,128]{2,1,0:T(8,128)} %get-tuple-element.23.cf, f32[3,288,128]{2,1,0:T(8,128)} %copy-done.1, s32[2]{0:T(128)} %fringe.3), custom_call_target="tpu_custom_call" | custom-call | tf_op jit(solution)/shard_map/pallas_call | solution.py:298
Async XLA Ops:
  1.9 13.4 %collective-permute-start = (f32[18,16,128]{2,1,0:T(8,128)}, f32[18,16,128]{2,1,0:T(8,128)S(1)}, u32[]{:S(2)}, u32[]{:S(2)}) collective-permute-start(f32[18,16,128]{2,1,0:T(8,128)} %get-tuple-element.15), channel_id=1, source_target_pairs={{0,1},{1,2},{2,3},{3,4},{4,5},{5,6},{6,7},{7,8},{8,9},{9,10},{10,1... | collective-permute-start | bytes 442376 | tf_op jit(solution)/shard_map/ppermute | solution.py:275
  5.9 11.0 %collective-permute-start.1 = (f32[18,16,128]{2,1,0:T(8,128)}, f32[18,16,128]{2,1,0:T(8,128)S(1)}, u32[]{:S(2)}, u32[]{:S(2)}) collective-permute-start(f32[18,16,128]{2,1,0:T(8,128)} %get-tuple-element.16), channel_id=1, source_target_pairs={{0,15},{1,0},{2,1},{3,2},{4,3},{5,4},{6,5},{7,6},{8,7},{9,8},{10,9... | collective-permute-start | bytes 442376 | tf_op jit(solution)/shard_map/ppermute | solution.py:276
  15.3 1.6 %copy-start.4 = (f32[18,16,128]{2,1,0:T(8,128)}, f32[18,16,128]{2,1,0:T(8,128)S(1)}, u32[]{:S(2)}) copy-start(f32[18,16,128]{2,1,0:T(8,128)S(1)} %collective-permute-done.lo) | copy-start | bytes 442372
  16.9 0.6 copy-start.5
  20.2 33.3 %collective-permute-start.4 = (f32[4,384,128]{2,1,0:T(8,128)}, f32[4,384,128]{2,1,0:T(8,128)S(1)}, u32[]{:S(2)}, u32[]{:S(2)}) collective-permute-start(f32[4,384,128]{2,1,0:T(8,128)} %get-tuple-element.18.a), channel_id=1, source_target_pairs={{0,512},{1,513},{2,514},{3,515},{4,516},{5,517},{6,518},{7,519},{8... | collective-permute-start | bytes 2359304 | tf_op jit(solution)/shard_map/ppermute | solution.py:283
  21.5 21.3 %collective-permute-start.2 = (f32[288,128]{1,0:T(8,128)}, f32[288,128]{1,0:T(8,128)S(1)}, u32[]{:S(2)}, u32[]{:S(2)}) collective-permute-start(f32[288,128]{1,0:T(8,128)} %get-tuple-element.20), channel_id=1, source_target_pairs={{0,16},{16,32},{32,48},{48,64},{64,80},{80,96},{96,112},{112,128},... | collective-permute-start | bytes 442376 | tf_op jit(solution)/shard_map/ppermute | solution.py:281
  32.6 20.9 %collective-permute-start.3 = (f32[288,128]{1,0:T(8,128)}, f32[288,128]{1,0:T(8,128)S(1)}, u32[]{:S(2)}, u32[]{:S(2)}) collective-permute-start(f32[288,128]{1,0:T(8,128)} %get-tuple-element.21), channel_id=1, source_target_pairs={{0,496},{16,0},{32,16},{48,32},{64,48},{80,64},{96,80},{112,96},{1... | collective-permute-start | bytes 442376 | tf_op jit(solution)/shard_map/ppermute | solution.py:282
  42.8 10.7 %copy-start.2 = (f32[288,128]{1,0:T(8,128)}, f32[288,128]{1,0:T(8,128)S(1)}, u32[]{:S(2)}) copy-start(f32[288,128]{1,0:T(8,128)S(1)} %collective-permute-done.2.lo) | copy-start | bytes 442372
  53.5 0.7 copy-start.3
  53.5 0.9 %copy-start = (f32[4,384,128]{2,1,0:T(8,128)}, f32[4,384,128]{2,1,0:T(8,128)S(1)}, u32[]{:S(2)}) copy-start(f32[4,384,128]{2,1,0:T(8,128)S(1)} %collective-permute-done.4.main_a) | copy-start | bytes 2359300
  61.8 3.9 %collective-permute-start.5 = (f32[3,288,128]{2,1,0:T(8,128)}, f32[3,288,128]{2,1,0:T(8,128)S(1)}, u32[]{:S(2)}, u32[]{:S(2)}) collective-permute-start(f32[3,288,128]{2,1,0:T(8,128)} %get-tuple-element.24), channel_id=1, source_target_pairs={{0,512},{1,513},{2,514},{3,515},{4,516},{5,517},{6,518},{7,519},{8... | collective-permute-start | bytes 1327112 | tf_op jit(solution)/shard_map/ppermute | solution.py:297
  65.7 0.8 %copy-start.1 = (f32[3,288,128]{2,1,0:T(8,128)}, f32[3,288,128]{2,1,0:T(8,128)S(1)}, u32[]{:S(2)}) copy-start(f32[3,288,128]{2,1,0:T(8,128)S(1)} %collective-permute-done.5.main_a) | copy-start | bytes 1327108

commit v2 on v1

v2 whole, which is shorter than its diff:
```python
import math

import jax
import jax.numpy as jnp
from jax import lax
from jax.experimental import pallas as pl
from jax.experimental.pallas import tpu as pltpu
from jax.sharding import PartitionSpec as P


DT = 0.1
HALF = 0.5 * DT
SMAG = 0.1
SOUND_SQ = 4.0
DRAG = 1.0
RATE = 3.0

T = 16
NZ = 128
R = 24
SPARE = 8
F32 = jnp.float32
VMEM = pl.BlockSpec(memory_space=pltpu.VMEM)
SMEM = pl.BlockSpec(memory_space=pltpu.SMEM)
HBM = pl.BlockSpec(memory_space=pltpu.HBM)

Y_WIND, Y_ADJ, Y_DRAG, Y_LEN = 0, 9, 17, 18
X_U1, X_U2, X_A1, X_A2, X_NU2, X_D1, X_LEN = 0, 60, 114, 186, 250, 266, 288
LEFT, RIGHT = 2, -8
KEPT = ((0, 1, 2), (13, 14, 15))


def shape(*dims):
    return jax.ShapeDtypeStruct(dims, F32)


def planes(n, *lead):
    return lead + (n * R + SPARE, NZ)


def call(body, outs, specs, scratch=(), flops=0):
    made = pl.pallas_call(
        body,
        out_shape=outs,
        in_specs=specs,
        out_specs=jax.tree.map(lambda _: VMEM, outs),
        scratch_shapes=scratch,
        compiler_params=pltpu.CompilerParams(vmem_limit_bytes=16 * 1024 * 1024),
        cost_estimate=pl.CostEstimate(flops=flops, bytes_accessed=0, transcendentals=0),
    )
    return made


def scratch(*dims):
    return pltpu.VMEM(dims, F32)


def is_main():
    return (lax.axis_index("dom") == 0).astype(F32)


def even(axis):
    return lax.rem(lax.axis_index(axis), 2) == 0


def up_z(v):
    return pltpu.roll(v, NZ - 1, 1)


def down_z(v):
    return pltpu.roll(v, 1, 1)


def edges_z(rows):
    lane = lax.broadcasted_iota(jnp.int32, (rows, NZ), 1)
    return (lane < NZ - 1).astype(F32), (lane > 0).astype(F32)


def drag_rows(u, v, w, turb):
    return (DT * DRAG) * turb * jnp.sqrt(u * u + v * v + w * w) * is_main()


def pack_y(w_hbm, a_hbm, t_hbm, first, second, w, a, t, sems):
    copies = [
        pltpu.make_async_copy(src, dst, sems.at[k])
        for k, (src, dst) in enumerate(((w_hbm, w), (a_hbm, a), (t_hbm, t)))
    ]
    for copy in copies:
        copy.start()
    sides = []
    for msg, top in ((first, even("gy")), (second, jnp.logical_not(even("gy")))):
        sides.append((msg, jnp.where(top, T - 3, 0), jnp.where(top, T - 2, 0), jnp.where(top, T - 1, 0)))
    copies[0].wait()
    for msg, edge, _, _ in sides:
        for c in range(3):
            for l in range(3):
                msg[Y_WIND + 3 * c + l] = w[c, pl.ds(edge + l, T, stride=T), :]
    copies[1].wait()
    for msg, _, edge, _ in sides:
        for c in range(4):
            for l in range(2):
                msg[Y_ADJ + 2 * c + l] = a[c, pl.ds(edge + l, T, stride=T), :]
    copies[2].wait()
    for msg, _, _, near in sides:
        u, v, z = (w[c, pl.ds(near, T, stride=T), :] for c in range(3))
        turb = t[pl.ds(near, T, stride=T), :].astype(F32)
        msg[Y_DRAG] = drag_rows(u, v, z, turb)


def y_rims(first, second, ew, ea, ed, shift, firsts, count):
    for msg, top in ((first, even("gy")), (second, jnp.logical_not(even("gy")))):
        base = (firsts + shift) * R
        at_w, at_a, at_d = (base + jnp.where(top, T + 3, k) for k in range(3))
        own = pl.ds(firsts, count)
        for c in range(3):
            for l in range(3):
                ew[c, pl.ds(at_w + l, count, stride=R), :] = msg[Y_WIND + 3 * c + l, own]
        for c in range(4):
            for l in range(2):
                ea[c, pl.ds(at_a + l, count, stride=R), :] = msg[Y_ADJ + 2 * c + l, own]
        ed[pl.ds(at_d, count, stride=R), :] = msg[Y_DRAG, own]


def own_rows(x, to, w, a, t, ew, ea, ed):
    wind = [w[c, pl.ds(x * T, T), :] for c in range(3)]
    for c in range(3):
        ew[c, pl.ds(to * R + 3, T), :] = wind[c]
    for c in range(4):
        ea[c, pl.ds(to * R + 3, T), :] = a[c, pl.ds(x * T, T), :]
    ed[pl.ds(to * R + 3, T), :] = drag_rows(*wind, t[pl.ds(x * T, T), :].astype(F32))


def spread_rows(w, a, t, first, second, ew, ea, ed, vel):
    for x in range(T):
        own_rows(x, x, w, a, t, ew, ea, ed)
    y_rims(first, second, ew, ea, ed, 0, 0, T)
    vel[...] = ea[pl.ds(0, 3), pl.ds(0, T * R), :]


def nu_rows(ew, at, rows, ones_p, ones_m):
    g = []
    for c in range(3):
        mid = ew[c, pl.ds(at, rows), :]
        gx = ew[c, pl.ds(at + R, rows), :] - ew[c, pl.ds(at - R, rows), :]
        gy = ew[c, pl.ds(at + 1, rows), :] - ew[c, pl.ds(at - 1, rows), :]
        gz = up_z(mid) * ones_p - down_z(mid) * ones_m
        g.append((gx, gy, gz))
    diag = g[0][0] * g[0][0] + g[1][1] * g[1][1] + g[2][2] * g[2][2]
    xy = g[1][0] + g[0][1]
    xz = g[2][0] + g[0][2]
    yz = g[2][1] + g[1][2]
    return SMAG * jnp.sqrt(0.5 * diag + 0.25 * (xy * xy + xz * xz + yz * yz))


def pack_x(w, a, t, first_y, second_y, first, second, ew, ea, ed):
    for x in KEPT[0] + KEPT[1]:
        own_rows(x, x if x < 8 else x - 10, w, a, t, ew, ea, ed)
    y_rims(first_y, second_y, ew, ea, ed, 0, 0, 3)
    y_rims(first_y, second_y, ew, ea, ed, -10, 13, 3)
    ones_p, ones_m = edges_z(T)
    for msg, top in ((first, even("gx")), (second, jnp.logical_not(even("gx")))):
        x1, x2 = jnp.where(top, 5 * R, 0), jnp.where(top, 4 * R, R)
        for c in range(3):
            msg[pl.ds(X_U1 + 20 * c, 20), :] = ew[c, pl.ds(x1 + 1, 20), :]
            msg[pl.ds(X_U2 + 18 * c, 18), :] = ew[c, pl.ds(x2 + 2, 18), :]
        for c in range(4):
            msg[pl.ds(X_A1 + 18 * c, 18), :] = ea[c, pl.ds(x1 + 2, 18), :]
            msg[pl.ds(X_A2 + 16 * c, 16), :] = ea[c, pl.ds(x2 + 3, 16), :]
        msg[pl.ds(X_NU2, 16), :] = HALF * nu_rows(ew, x2 + 3, T, ones_p, ones_m)
        msg[pl.ds(X_D1, 16), :] = ed[pl.ds(x1 + 3, 16), :]
        msg[pl.ds(X_D1 + 16, 6), :] = jnp.zeros((6, NZ), F32)


def fringe_table(fringe, table):
    total = T * lax.axis_size("gx")
    x = lax.broadcasted_iota(jnp.int32, (R, NZ), 0) - 1
    place = lax.axis_index("gx") * T + x - fringe[0]
    offset = lax.rem(place + 2 * total, jnp.full_like(place, total))
    width = fringe[1]
    phase = (math.pi * (offset.astype(F32) + 0.5)) / jnp.full((R, NZ), width, jnp.int32).astype(F32)
    sine = jnp.sin(phase)
    table[...] = jnp.where(offset < width, (DT * RATE) * (sine * sine), 0.0)


def rate_rows(table, x, rows):
    return jnp.broadcast_to(table[pl.ds(x + 1, 1), :], (rows, NZ))


def coefficients(nu, at, wind, lost, ones_p, ones_m):
    h = nu[pl.ds(at, R), :]
    hxp, hxm = nu[pl.ds(at + R, R), :], nu[pl.ds(at - R, R), :]
    hyp, hym = nu[pl.ds(at + 1, R), :], nu[pl.ds(at - 1, R), :]
    hzp, hzm = up_z(h) * ones_p, down_z(h) * ones_m
    pu, pv, pw = (HALF * v for v in wind)
    return (
        (1.0 - lost) - (6.0 * h + (hxp + hxm) + (hyp + hym) + (hzp + hzm)),
        h + hxp + pu,
        h + hxm - pu,
        h + hyp + pv,
        h + hym - pv,
        (h + hzp + pw) * ones_p,
        (h + hzm - pw) * ones_m,
    )


def stencil(a, at, rows, coefs, wind, ones_p, ones_m):
    c0, cxp, cxm, cyp, cym, czp, czm = coefs
    new, dx, dy, dz = [], [], [], []
    for c in range(4):
        mid = a[c, pl.ds(at, rows), :]
        xp, xm = a[c, pl.ds(at + R, rows), :], a[c, pl.ds(at - R, rows), :]
        yp, ym = a[c, pl.ds(at + 1, rows), :], a[c, pl.ds(at - 1, rows), :]
        zp, zm = up_z(mid), down_z(mid)
        if c < 3:
            new.append(c0 * mid + (cxp * xp + cxm * xm) + (cyp * yp + cym * ym) + (czp * zp + czm * zm))
        else:
            new.append(mid)
        dx.append(xp - xm if c in (0, 3) else None)
        dy.append(yp - ym if c in (1, 3) else None)
        dz.append(zp * ones_p - zm * ones_m if c in (2, 3) else None)
    sound = HALF * SOUND_SQ
    new[0] = new[0] + sound * dx[3]
    new[1] = new[1] + sound * dy[3]
    new[2] = new[2] + sound * dz[3]
    u, v, w = wind
    new[3] = new[3] + HALF * (u * dx[3] + v * dy[3] + w * dz[3] + dx[0] + dy[1] + dz[2])
    return new


def second_plane(own, at, cf_at, to, w, a1, cf, out, ones_p, ones_m):
    wind = [w[c, pl.ds(own, T), :] for c in range(3)]
    coefs = [cf[k, pl.ds(cf_at, T), :] for k in range(7)]
    new = stencil(a1, at, T, coefs, wind, ones_p, ones_m)
    for c in range(4):
        out[c, pl.ds(to, T), :] = new[c]


def inner(w, ew, ea, ed, main_a, fringe, nu, cf, a1, out, table):
    main = is_main()
    fringe_table(fringe, table)
    ones_p, ones_m = edges_z(R)

    def nu_plane(x, _):
        at = pl.multiple_of(x * R, 8)
        nu[pl.ds(at, R), :] = HALF * nu_rows(ew, at, R, ones_p, ones_m)
        return 0

    lax.fori_loop(1, T - 1, nu_plane, 0)

    def plane(x, _):
        at = pl.multiple_of(x * R, 8)
        wind = [ew[c, pl.ds(at, R), :] for c in range(3)]
        rate = rate_rows(table, x, R)
        coefs = coefficients(nu, at, wind, ed[pl.ds(at, R), :] + main * rate, ones_p, ones_m)
        new = stencil(ea, at, R, coefs, wind, ones_p, ones_m)
        push = (1.0 - main) * rate
        for c in range(4):
            a1[c, pl.ds(at, R), :] = new[c] if c == 3 else new[c] + push * main_a[c, pl.ds(at, R), :]
        for k in range(7):
            cf[k, pl.ds(at, R), :] = coefs[k]
        return 0

    lax.fori_loop(2, T - 2, plane, 0)
    short_p, short_m = edges_z(T)

    def later(x, _):
        own, at = pl.multiple_of(x * T, 8), x * R + 3
        second_plane(own, at, at, own, w, a1, cf, out, short_p, short_m)
        return 0

    lax.fori_loop(3, T - 3, later, 0)


def edges(first, second, ew, ea, ed, nu, main_a, table, cf_in, a1_in, cf, a1, sent, sw, sa, sd, sn):
    main = is_main()
    for group, shift in zip(KEPT, (LEFT, RIGHT)):
        for x in group:
            at, to = x * R, (x + shift) * R
            for c in range(3):
                sw[c, pl.ds(to, R), :] = ew[c, pl.ds(at, R), :]
            for c in range(4):
                sa[c, pl.ds(to, R), :] = ea[c, pl.ds(at, R), :]
            sd[pl.ds(to, R), :] = ed[pl.ds(at, R), :]
            sn[pl.ds(to, R), :] = nu[pl.ds(at, R), :]
    for msg, top in ((first, even("gx")), (second, jnp.logical_not(even("gx")))):
        p1, p2 = jnp.where(top, 8 * R, R), jnp.where(top, 9 * R, 0)
        for c in range(3):
            sw[c, pl.ds(p1 + 1, 20), :] = msg[pl.ds(X_U1 + 20 * c, 20), :]
            sw[c, pl.ds(p2 + 2, 18), :] = msg[pl.ds(X_U2 + 18 * c, 18), :]
        for c in range(4):
            sa[c, pl.ds(p1 + 2, 18), :] = msg[pl.ds(X_A1 + 18 * c, 18), :]
            sa[c, pl.ds(p2 + 3, 16), :] = msg[pl.ds(X_A2 + 16 * c, 16), :]
        sn[pl.ds(p2 + 3, 16), :] = msg[pl.ds(X_NU2, 16), :]
        sd[pl.ds(p1 + 3, 16), :] = msg[pl.ds(X_D1, 16), :]
    ones_p, ones_m = edges_z(R)

    def nu_plane(k, _):
        at = pl.multiple_of(jnp.where(k < 2, k + 1, k + 5) * R, 8)
        sn[pl.ds(at, R), :] = HALF * nu_rows(sw, at, R, ones_p, ones_m)
        return 0

    lax.fori_loop(0, 4, nu_plane, 0)

    def plane(k, _):
        p = jnp.where(k < 3, k + 1, k + 3)
        x = jnp.where(k < 3, k - 1, k + 11)
        at = pl.multiple_of(p * R, 8)
        to = pl.multiple_of(jnp.where(k < 3, k, k + 4) * R, 8)
        own = pl.multiple_of(jnp.clip(x, 0, T - 1) * R, 8)
        wind = [sw[c, pl.ds(at, R), :] for c in range(3)]
        rate = rate_rows(table, x, R)
        coefs = coefficients(sn, at, wind, sd[pl.ds(at, R), :] + main * rate, ones_p, ones_m)
        new = stencil(sa, at, R, coefs, wind, ones_p, ones_m)
        inside = jnp.logical_and(x >= 0, x < T).astype(F32)
        push = ((1.0 - main) * inside) * rate
        for c in range(4):
            a1[c, pl.ds(to, R), :] = new[c] if c == 3 else new[c] + push * main_a[c, pl.ds(own, R), :]
        keep = pl.multiple_of(jnp.where(k == 0, 6, jnp.where(k == 5, 7, jnp.where(k < 3, k - 1, k + 1))) * R, 8)
        for n in range(7):
            cf[n, pl.ds(keep, R), :] = coefs[n]
        return 0

    lax.fori_loop(0, 6, plane, 0)
    for x, p in ((2, 3), (3, 4), (12, 5), (13, 6)):
        for c in range(4):
            a1[c, pl.ds(p * R, R), :] = a1_in[c, pl.ds(x * R, R), :]
    for x, p in ((2, 2), (13, 3)):
        for n in range(7):
            cf[n, pl.ds(p * R, R), :] = cf_in[n, pl.ds(x * R, R), :]
    for c in range(3):
        sent[c, pl.ds(0, T), :] = sa[c, pl.ds(R + 3, T), :]
        for x in range(T):
            src = a1[c, pl.ds((x + 1 if x < 8 else x - 7) * R + 3, T), :] if x in (0, 1, 14, 15) else a1_in[
                c, pl.ds(x * R + 3, T), :
            ]
            sent[c, pl.ds((x + 1) * T, T), :] = src
        sent[c, pl.ds((T + 1) * T, T), :] = sa[c, pl.ds(8 * R + 3, T), :]


def second_edges(w, a1, cf, part):
    ones_p, ones_m = edges_z(T)

    def plane(k, _):
        x = jnp.where(k < 3, k, k + 10)
        p = jnp.where(k < 3, k + 1, k + 3)
        second_plane(pl.multiple_of(x * T, 8), p * R + 3, k * R + 3, pl.multiple_of(k * T, 8), w, a1, cf, part, ones_p, ones_m)
        return 0

    lax.fori_loop(0, 6, plane, 0)


def finish(part, part_edges, cf, main_a, table, out):
    other = 1.0 - is_main()
    for x in range(T):
        inside = 3 <= x < T - 3
        k = x if x < 8 else x - 10
        rate = rate_rows(table, x, T) * other
        src, at = (part, x * T) if inside else (part_edges, k * T)
        new = [src[c, pl.ds(at, T), :] for c in range(4)]
        for c in range(3):
            new[c] = new[c] + rate * main_a[c, pl.ds((x + 1) * T, T), :]
        if x in (0, T - 1):
            p, n, sign = (0, 2, -1.0) if x == 0 else (T + 1, 1, 1.0)
            rate = rate_rows(table, p - 1, T) * other
            beside = [rate * main_a[c, pl.ds(p * T, T), :] for c in range(3)]
            coef = cf[n, pl.ds(k * R + 3, T), :]
            for c in range(3):
                new[c] = new[c] + coef * beside[c]
            new[3] = new[3] + (sign * HALF) * beside[0]
        for c in range(4):
            out[c, pl.ds(x * T, T), :] = new[c]


def pairs(axis, offset):
    devices = lax.axis_size(axis)
    found = []
    for i in range(offset, devices + offset, 2):
        a, b = i % devices, (i + 1) % devices
        found += [(a, b), (b, a)]
    return found


def swap(first, second, axis):
    first = lax.ppermute(first, axis, pairs(axis, 0))
    second = lax.ppermute(second, axis, pairs(axis, 1))
    return first, second


def on_device(wind, adjoint, turbines, fringe_range):
    y_msg, x_msg = shape(Y_LEN, T, NZ), shape(X_LEN, NZ)
    tile = shape(4, T * T, NZ)
    y1, y2, w, a, t = call(
        pack_y,
        (y_msg, y_msg, shape(3, T * T, NZ), tile, jax.ShapeDtypeStruct((T * T, NZ), jnp.int32)),
        [HBM] * 3,
        scratch=[pltpu.SemaphoreType.DMA((3,))],
    )(
        *(
            pltpu.with_memory_space_constraint(v, pltpu.HBM)
            for v in (wind.reshape(3, T * T, NZ), adjoint.reshape(4, T * T, NZ), turbines.reshape(T * T, NZ))
        )
    )
    y1, y2 = swap(y1, y2, "gy")
    x1, x2 = call(
        pack_x,
        (x_msg, x_msg),
        [VMEM] * 5,
        scratch=[scratch(*planes(6, 3)), scratch(*planes(6, 4)), scratch(*planes(6))],
    )(w, a, t, y1, y2)
    x1, x2 = swap(x1, x2, "gx")
    ew, ea, ed, vel = call(
        spread_rows,
        (shape(*planes(T, 3)), shape(*planes(T, 4)), shape(*planes(T)), shape(3, T * R, NZ)),
        [VMEM] * 5,
        flops=10**6,
    )(w, a, t, y1, y2)
    main_a = lax.ppermute(vel, "dom", [(0, 1)])
    nu, cf, a1, part, table = call(
        inner,
        (shape(*planes(T)), shape(*planes(T, 7)), shape(*planes(T, 4)), tile, shape(R, NZ)),
        [VMEM] * 5 + [SMEM],
        flops=10**7,
    )(w, ew, ea, ed, main_a, fringe_range)
    cf_edges, a1_edges, sent = call(
        edges,
        (shape(*planes(8, 7)), shape(*planes(10, 4)), shape(3, (T + 2) * T, NZ)),
        [VMEM] * 10,
        scratch=[scratch(*planes(10, 3)), scratch(*planes(10, 4)), scratch(*planes(10)), scratch(*planes(10))],
    )(x1, x2, ew, ea, ed, nu, main_a, table, cf, a1)
    main_a1 = lax.ppermute(sent, "dom", [(0, 1)])
    part_edges = call(second_edges, shape(4, 6 * T, NZ), [VMEM] * 3, flops=10**6)(w, a1_edges, cf_edges)
    out = call(finish, tile, [VMEM] * 5)(part, part_edges, cf_edges, main_a1, table)
    return out.reshape(1, 4, T, T, NZ)


def solution(mesh):
    in_specs = (
        P("dom", None, "gx", "gy", None),
        P("dom", None, "gx", "gy", None),
        P("gx", "gy", None),
        P(),
    )
    out_specs = P("dom", None, "gx", "gy", None)
    return jax.shard_map(on_device, mesh=mesh, in_specs=in_specs, out_specs=out_specs, check_vma=False)
```

time: 71.1 us -> 59.5 us (0.84)
  Pallas kernels: 16.2 us -> 8.52 us
  waiting for transfers between devices: 16.6 us -> 12.1 us
  starting transfers between devices: 35.4 us -> 38.4 us
  local copies, waits for them, and re-layouts: 2.37 us -> 0.01 us
    pallas_call x4 -> x7, Pallas kernels: 16.2 us -> 8.52 us  [the longest x1 4.35 us: on_device(): call(inner, (shape(*planes(T)), shape(*planes(T, 7)), shape(*planes(T, 4)...]
    ppermute x5, waiting for transfers between devices: 14 us -> 10.3 us  [the longest x2 10.3 us: swap(): second = lax.ppermute(second, axis, pairs(axis, 1))]
    ppermute x5, starting transfers between devices: 34.2 us -> 37.1 us  [the longest x2 20.5 us: swap(): second = lax.ppermute(second, axis, pairs(axis, 1))]
    unnamed x12 -> x2, local copies, waits for them, and re-layouts: 2.37 us -> 0.01 us
    ppermute x1, waiting for transfers between devices: 2.6 us -> 1.84 us  [on_device(): main_a1 = lax.ppermute(sent, 'dom', [(0, 1)])]
  transfers between devices with their start and end apart: 6 -> 6, of which waited for: 5 -> 3; matrix products, arithmetic and copies ran while one was open for 0% -> 0% of each run, Pallas kernels for 0% -> 9%
where the time goes in v2:
time: 59.5 us; the launch traced here: 59.2 us
  starting transfers between devices  38.4 us (65%)
  waiting for transfers between devices  12.1 us (20%)
  Pallas kernels  8.52 us (14%)
    ppermute x2, starting transfers between devices, swap(): second = lax.ppermute(second, axis, pairs(axis, 1))  20.5 us
    ppermute x2, starting transfers between devices, swap(): first = lax.ppermute(first, axis, pairs(axis, 0))  15.3 us
    ppermute x2, waiting for transfers between devices, swap(): second = lax.ppermute(second, axis, pairs(axis, 1))  10.3 us
    pallas_call x1, Pallas kernels, on_device(): call(inner, (shape(*planes(T)), shape(*planes(T, 7)), shape(*planes(T, 4)...  4.35 us
    ppermute x1, waiting for transfers between devices, on_device(): main_a1 = lax.ppermute(sent, 'dom', [(0, 1)])  1.84 us
    ppermute x1, starting transfers between devices, on_device(): main_a = lax.ppermute(vel, 'dom', [(0, 1)])  1.29 us
    ppermute x1, starting transfers between devices, on_device(): main_a1 = lax.ppermute(sent, 'dom', [(0, 1)])  1.29 us
    pallas_call x1, Pallas kernels, on_device(): call(pack_y, (y_msg, y_msg, shape(3, T * T, NZ), tile, jax.ShapeDtypeStru...  1.28 us
  transfers between devices with their start and end apart: 6, of which 3 were waited for; matrix products, arithmetic and copies ran while one was open for 0% of the time, Pallas kernels for 9%

profile of v2, /device:TPU:1, one launch (start us, length us, event | category | flops | bytes accessed | tf_op | source)
XLA Modules:
  0.0 59.2 jit_solution(2632823784088492123)
XLA Ops:
  0.0 1.3 %shard_map.46 = (f32[18,16,128]{2,1,0:T(8,128)S(1)}, f32[18,16,128]{2,1,0:T(8,128)S(1)}, f32[3,256,128]{2,1,0:T(8,128)S(1)}, f32[4,256,128]{2,1,0:T(8,128)S(1)}, s32[256,128]{1,0:T(8,128)S(1)}) custom-call(f32[3,256,128]{2,1,0:T(8,128)} %bitcast.5, f32[4,256,128]{2,1,0:T(8,128)} %bitcast.4, s32[256,128]{1,0:T(8,128)} %bitcast.6), custom_call_target="tpu_custom_call" | custom-call | tf_op jit(solution)/shard_map/pallas_call | solution.py:392
  1.3 0.0 copy-start
  1.3 3.9 %collective-permute-start = (f32[18,16,128]{2,1,0:T(8,128)S(1)}, f32[18,16,128]{2,1,0:T(8,128)S(1)}, u32[]{:S(2)}, u32[]{:S(2)}) collective-permute-start(f32[18,16,128]{2,1,0:T(8,128)S(1)} %get-tuple-element.27), channel_id=1, source_target_pairs={{0,1},{1,0},{2,3},{3,2},{4,5},{5,4},{6,7},{7,6},{8,9},{9,8},{10,11... | collective-permute-start | bytes 442376 | tf_op jit(solution)/shard_map/ppermute | solution.py:384
  5.2 9.1 %collective-permute-start.1 = (f32[18,16,128]{2,1,0:T(8,128)S(1)}, f32[18,16,128]{2,1,0:T(8,128)S(1)}, u32[]{:S(2)}, u32[]{:S(2)}) collective-permute-start(f32[18,16,128]{2,1,0:T(8,128)S(1)} %get-tuple-element.28), channel_id=1, source_target_pairs={{1,2},{2,1},{3,4},{4,3},{5,6},{6,5},{7,8},{8,7},{9,10},{10,9},{11,... | collective-permute-start | bytes 442376 | tf_op jit(solution)/shard_map/ppermute | solution.py:385
  14.4 0.0 collective-permute-done.first.first_y
  14.4 2.5 %collective-permute-done.1.second.second_y = f32[18,16,128]{2,1,0:T(8,128)S(1)} collective-permute-done((f32[18,16,128]{2,1,0:T(8,128)S(1)}, f32[18,16,128]{2,1,0:T(8,128)S(1)}, u32[]{:S(2)}, u32[]{:S(2)}) %collective-permute-start.1) | collective-permute-done | bytes 147488 | tf_op jit(solution)/shard_map/ppermute | solution.py:385
  16.9 0.2 shard_map.47
  17.1 1.3 %collective-permute-start.2 = (f32[3,384,128]{2,1,0:T(8,128)S(1)}, f32[3,384,128]{2,1,0:T(8,128)S(1)}, u32[]{:S(2)}, u32[]{:S(2)}) collective-permute-start(f32[3,384,128]{2,1,0:T(8,128)S(1)} %get-tuple-element.32), channel_id=1, source_target_pairs={{0,512},{1,513},{2,514},{3,515},{4,516},{5,517},{6,518},{7,519},{8... | collective-permute-start | bytes 1769480 | tf_op jit(solution)/shard_map/ppermute | solution.py:417
  18.4 0.2 shard_map.49
  18.5 11.4 %collective-permute-start.3 = (f32[288,128]{1,0:T(8,128)S(1)}, f32[288,128]{1,0:T(8,128)S(1)}, u32[]{:S(2)}, u32[]{:S(2)}) collective-permute-start(f32[288,128]{1,0:T(8,128)S(1)} %get-tuple-element.34), channel_id=1, source_target_pairs={{0,16},{16,0},{32,48},{48,32},{64,80},{80,64},{96,112},{112,96},{1... | collective-permute-start | bytes 442376 | tf_op jit(solution)/shard_map/ppermute | solution.py:384
  29.9 11.4 %collective-permute-start.4 = (f32[288,128]{1,0:T(8,128)S(1)}, f32[288,128]{1,0:T(8,128)S(1)}, u32[]{:S(2)}, u32[]{:S(2)}) collective-permute-start(f32[288,128]{1,0:T(8,128)S(1)} %get-tuple-element.35), channel_id=1, source_target_pairs={{16,32},{32,16},{48,64},{64,48},{80,96},{96,80},{112,128},{128,112... | collective-permute-start | bytes 442376 | tf_op jit(solution)/shard_map/ppermute | solution.py:385
  41.3 0.0 collective-permute-done.2.main_a
  41.3 0.0 copy-done
  41.3 4.3 %shard_map.48 = (f32[392,128]{1,0:T(8,128)S(1)}, f32[7,392,128]{2,1,0:T(8,128)S(1)}, f32[4,392,128]{2,1,0:T(8,128)S(1)}, f32[4,256,128]{2,1,0:T(8,128)S(1)}, f32[24,128]{1,0:T(8,128)S(1)}) custom-call(f32[3,256,128]{2,1,0:T(8,128)S(1)} %get-tuple-element.24.w, f32[3,392,128]{2,1,0:T(8,128)S(1)} %get-tuple-element.29.ew, ...), custom_call_target="tpu_custom_call" | custom-call | flops 10000000 | tf_op jit(solution)/shard_map/pallas_call | solution.py:418
  45.7 0.0 collective-permute-done.3.first
  45.7 7.8 %collective-permute-done.4.second = f32[288,128]{1,0:T(8,128)S(1)} collective-permute-done((f32[288,128]{1,0:T(8,128)S(1)}, f32[288,128]{1,0:T(8,128)S(1)}, u32[]{:S(2)}, u32[]{:S(2)}) %collective-permute-start.4) | collective-permute-done | bytes 147488 | tf_op jit(solution)/shard_map/ppermute | solution.py:385
  53.5 1.2 %shard_map.50 = (f32[7,200,128]{2,1,0:T(8,128)S(1)}, f32[4,248,128]{2,1,0:T(8,128)S(1)}, f32[3,288,128]{2,1,0:T(8,128)S(1)}) custom-call(f32[288,128]{1,0:T(8,128)S(1)} %collective-permute-done.3.first, f32[288,128]{1,0:T(8,128)S(1)} %collective-permute-done.4.second, f32[3,392,128]{2,1,0:T(8,128)S(1)} %get-tuple-element.29.ew, ...), custom_call_target="tpu_custom_call" | custom-call | tf_op jit(solution)/shard_map/pallas_call | solution.py:424
  54.6 1.3 %collective-permute-start.5 = (f32[3,288,128]{2,1,0:T(8,128)S(1)}, f32[3,288,128]{2,1,0:T(8,128)S(1)}, u32[]{:S(2)}, u32[]{:S(2)}) collective-permute-start(f32[3,288,128]{2,1,0:T(8,128)S(1)} %get-tuple-element.42), channel_id=1, source_target_pairs={{0,512},{1,513},{2,514},{3,515},{4,516},{5,517},{6,518},{7,519},{8... | collective-permute-start | bytes 1327112 | tf_op jit(solution)/shard_map/ppermute | solution.py:430
  55.9 0.5 shard_map.51.part_edges
  56.5 1.8 %collective-permute-done.5.main_a = f32[3,288,128]{2,1,0:T(8,128)S(1)} collective-permute-done((f32[3,288,128]{2,1,0:T(8,128)S(1)}, f32[3,288,128]{2,1,0:T(8,128)S(1)}, u32[]{:S(2)}, u32[]{:S(2)}) %collective-permute-start.5) | collective-permute-done | bytes 442400 | tf_op jit(solution)/shard_map/ppermute | solution.py:430
  58.3 0.9 %shard_map.52 = f32[4,256,128]{2,1,0:T(8,128)} custom-call(f32[4,256,128]{2,1,0:T(8,128)S(1)} %get-tuple-element.33.part, f32[4,96,128]{2,1,0:T(8,128)S(1)} %shard_map.51.part_edges, f32[7,200,128]{2,1,0:T(8,128)S(1)} %get-tuple-element.41.cf, f32[3,288,128]{2,1,0:T(8,128)S(1)} %collective-permute-done.5.main_a, f32[24,128]{1,0:T(8,128)S(1)} %get-tuple-element.37.table), custom_call_target="tpu_custom_call" | custom-call | tf_op jit(solution)/shard_map/pallas_call | solution.py:432
Async XLA Ops:
  1.3 40.0 %copy-start = (s32[2]{0:T(128)S(1)}, s32[2]{0:T(128)}, u32[]{:S(2)}) copy-start(s32[2]{0:T(128)} %fringe.1) | copy-start | bytes 28
  1.3 13.1 %collective-permute-start = (f32[18,16,128]{2,1,0:T(8,128)S(1)}, f32[18,16,128]{2,1,0:T(8,128)S(1)}, u32[]{:S(2)}, u32[]{:S(2)}) collective-permute-start(f32[18,16,128]{2,1,0:T(8,128)S(1)} %get-tuple-element.27), channel_id=1, source_target_pairs={{0,1},{1,0},{2,3},{3,2},{4,5},{5,4},{6,7},{7,6},{8,9},{9,8},{10,11... | collective-permute-start | bytes 442376 | tf_op jit(solution)/shard_map/ppermute | solution.py:384
  5.2 11.7 %collective-permute-start.1 = (f32[18,16,128]{2,1,0:T(8,128)S(1)}, f32[18,16,128]{2,1,0:T(8,128)S(1)}, u32[]{:S(2)}, u32[]{:S(2)}) collective-permute-start(f32[18,16,128]{2,1,0:T(8,128)S(1)} %get-tuple-element.28), channel_id=1, source_target_pairs={{1,2},{2,1},{3,4},{4,3},{5,6},{6,5},{7,8},{8,7},{9,10},{10,9},{11,... | collective-permute-start | bytes 442376 | tf_op jit(solution)/shard_map/ppermute | solution.py:385
  17.1 24.2 %collective-permute-start.2 = (f32[3,384,128]{2,1,0:T(8,128)S(1)}, f32[3,384,128]{2,1,0:T(8,128)S(1)}, u32[]{:S(2)}, u32[]{:S(2)}) collective-permute-start(f32[3,384,128]{2,1,0:T(8,128)S(1)} %get-tuple-element.32), channel_id=1, source_target_pairs={{0,512},{1,513},{2,514},{3,515},{4,516},{5,517},{6,518},{7,519},{8... | collective-permute-start | bytes 1769480 | tf_op jit(solution)/shard_map/ppermute | solution.py:417
  18.5 27.2 %collective-permute-start.3 = (f32[288,128]{1,0:T(8,128)S(1)}, f32[288,128]{1,0:T(8,128)S(1)}, u32[]{:S(2)}, u32[]{:S(2)}) collective-permute-start(f32[288,128]{1,0:T(8,128)S(1)} %get-tuple-element.34), channel_id=1, source_target_pairs={{0,16},{16,0},{32,48},{48,32},{64,80},{80,64},{96,112},{112,96},{1... | collective-permute-start | bytes 442376 | tf_op jit(solution)/shard_map/ppermute | solution.py:384
  29.9 23.5 %collective-permute-start.4 = (f32[288,128]{1,0:T(8,128)S(1)}, f32[288,128]{1,0:T(8,128)S(1)}, u32[]{:S(2)}, u32[]{:S(2)}) collective-permute-start(f32[288,128]{1,0:T(8,128)S(1)} %get-tuple-element.35), channel_id=1, source_target_pairs={{16,32},{32,16},{48,64},{64,48},{80,96},{96,80},{112,128},{128,112... | collective-permute-start | bytes 442376 | tf_op jit(solution)/shard_map/ppermute | solution.py:385
  54.6 3.7 %collective-permute-start.5 = (f32[3,288,128]{2,1,0:T(8,128)S(1)}, f32[3,288,128]{2,1,0:T(8,128)S(1)}, u32[]{:S(2)}, u32[]{:S(2)}) collective-permute-start(f32[3,288,128]{2,1,0:T(8,128)S(1)} %get-tuple-element.42), channel_id=1, source_target_pairs={{0,512},{1,513},{2,514},{3,515},{4,516},{5,517},{6,518},{7,519},{8... | collective-permute-start | bytes 1327112 | tf_op jit(solution)/shard_map/ppermute | solution.py:430

commit v3 on v2

--- a/solution.py
+++ b/solution.py
@@ -59,8 +59,12 @@
     return (lax.axis_index("dom") == 0).astype(F32)
 
 
-def even(axis):
-    return lax.rem(lax.axis_index(axis), 2) == 0
+def sends_up():
+    return True, False
+
+
+def from_above():
+    return False, True
 
 
 def up_z(v):
@@ -88,7 +92,7 @@
     for copy in copies:
         copy.start()
     sides = []
-    for msg, top in ((first, even("gy")), (second, jnp.logical_not(even("gy")))):
+    for msg, top in zip((first, second), sends_up()):
         sides.append((msg, jnp.where(top, T - 3, 0), jnp.where(top, T - 2, 0), jnp.where(top, T - 1, 0)))
     copies[0].wait()
     for msg, edge, _, _ in sides:
@@ -108,7 +112,7 @@
 
 
 def y_rims(first, second, ew, ea, ed, shift, firsts, count):
-    for msg, top in ((first, even("gy")), (second, jnp.logical_not(even("gy")))):
+    for msg, top in zip((first, second), from_above()):
         base = (firsts + shift) * R
         at_w, at_a, at_d = (base + jnp.where(top, T + 3, k) for k in range(3))
         own = pl.ds(firsts, count)
@@ -158,7 +162,7 @@
     y_rims(first_y, second_y, ew, ea, ed, 0, 0, 3)
     y_rims(first_y, second_y, ew, ea, ed, -10, 13, 3)
     ones_p, ones_m = edges_z(T)
-    for msg, top in ((first, even("gx")), (second, jnp.logical_not(even("gx")))):
+    for msg, top in zip((first, second), sends_up()):
         x1, x2 = jnp.where(top, 5 * R, 0), jnp.where(top, 4 * R, R)
         for c in range(3):
             msg[pl.ds(X_U1 + 20 * c, 20), :] = ew[c, pl.ds(x1 + 1, 20), :]
@@ -282,7 +286,7 @@
                 sa[c, pl.ds(to, R), :] = ea[c, pl.ds(at, R), :]
             sd[pl.ds(to, R), :] = ed[pl.ds(at, R), :]
             sn[pl.ds(to, R), :] = nu[pl.ds(at, R), :]
-    for msg, top in ((first, even("gx")), (second, jnp.logical_not(even("gx")))):
+    for msg, top in zip((first, second), from_above()):
         p1, p2 = jnp.where(top, 8 * R, R), jnp.where(top, 9 * R, 0)
         for c in range(3):
             sw[c, pl.ds(p1 + 1, 20), :] = msg[pl.ds(X_U1 + 20 * c, 20), :]
@@ -371,18 +375,14 @@
             out[c, pl.ds(x * T, T), :] = new[c]
 
 
-def pairs(axis, offset):
+def ring(axis, by):
     devices = lax.axis_size(axis)
-    found = []
-    for i in range(offset, devices + offset, 2):
-        a, b = i % devices, (i + 1) % devices
-        found += [(a, b), (b, a)]
-    return found
-
-
-def swap(first, second, axis):
-    first = lax.ppermute(first, axis, pairs(axis, 0))
-    second = lax.ppermute(second, axis, pairs(axis, 1))
+    return [(i, (i + by) % devices) for i in range(devices)]
+
+
+def exchange(first, second, axis):
+    first = lax.ppermute(first, axis, ring(axis, 1))
+    second = lax.ppermute(second, axis, ring(axis, -1))
     return first, second
 
 
@@ -400,14 +400,14 @@
             for v in (wind.reshape(3, T * T, NZ), adjoint.reshape(4, T * T, NZ), turbines.reshape(T * T, NZ))
         )
     )
-    y1, y2 = swap(y1, y2, "gy")
+    y1, y2 = exchange(y1, y2, "gy")
     x1, x2 = call(
         pack_x,
         (x_msg, x_msg),
         [VMEM] * 5,
         scratch=[scratch(*planes(6, 3)), scratch(*planes(6, 4)), scratch(*planes(6))],
     )(w, a, t, y1, y2)
-    x1, x2 = swap(x1, x2, "gx")
+    x1, x2 = exchange(x1, x2, "gx")
     ew, ea, ed, vel = call(
         spread_rows,
         (shape(*planes(T, 3)), shape(*planes(T, 4)), shape(*planes(T)), shape(3, T * R, NZ)),

time: 59.5 us -> 55.2 us (0.928)
  starting transfers between devices: 38.4 us -> 35.3 us
  waiting for transfers between devices: 12.1 us -> 11 us
    ppermute x4, starting transfers between devices: 35.8 us -> 32.7 us  [the longest x2 17.7 us: exchange(): second = lax.ppermute(second, axis, ring(axis, -1))]
    ppermute x4, waiting for transfers between devices: 10.3 us -> 9.16 us  [the longest x2 8.57 us: exchange(): second = lax.ppermute(second, axis, ring(axis, -1))]
  transfers between devices with their start and end apart: 6 -> 6, of which waited for: 3 -> 4; matrix products, arithmetic and copies ran while one was open for 0% -> 0% of each run, Pallas kernels for 9% -> 9%
where the time goes in v3:
time: 55.2 us; the launch traced here: 54.9 us
  starting transfers between devices  35.3 us (64%)
  waiting for transfers between devices  11 us (20%)
  Pallas kernels  8.47 us (15%)
    ppermute x2, starting transfers between devices, exchange(): second = lax.ppermute(second, axis, ring(axis, -1))  17.7 us
    ppermute x2, starting transfers between devices, exchange(): first = lax.ppermute(first, axis, ring(axis, 1))  15 us
    ppermute x2, waiting for transfers between devices, exchange(): second = lax.ppermute(second, axis, ring(axis, -1))  8.57 us
    pallas_call x1, Pallas kernels, on_device(): call(inner, (shape(*planes(T)), shape(*planes(T, 7)), shape(*planes(T, 4)...  4.35 us
    ppermute x1, waiting for transfers between devices, on_device(): main_a1 = lax.ppermute(sent, 'dom', [(0, 1)])  1.84 us
    ppermute x1, starting transfers between devices, on_device(): main_a = lax.ppermute(vel, 'dom', [(0, 1)])  1.29 us
    ppermute x1, starting transfers between devices, on_device(): main_a1 = lax.ppermute(sent, 'dom', [(0, 1)])  1.29 us
    pallas_call x1, Pallas kernels, on_device(): call(pack_y, (y_msg, y_msg, shape(3, T * T, NZ), tile, jax.ShapeDtypeStru...  1.27 us
  transfers between devices with their start and end apart: 6, of which 4 were waited for; matrix products, arithmetic and copies ran while one was open for 0% of the time, Pallas kernels for 9%

profile of v3, /device:TPU:1, one launch (start us, length us, event | category | flops | bytes accessed | tf_op | source)
XLA Modules:
  0.0 54.9 jit_solution(3803129377870635572)
XLA Ops:
  0.0 1.3 %shard_map.46 = (f32[18,16,128]{2,1,0:T(8,128)S(1)}, f32[18,16,128]{2,1,0:T(8,128)S(1)}, f32[3,256,128]{2,1,0:T(8,128)S(1)}, f32[4,256,128]{2,1,0:T(8,128)S(1)}, s32[256,128]{1,0:T(8,128)S(1)}) custom-call(f32[3,256,128]{2,1,0:T(8,128)} %bitcast.5, f32[4,256,128]{2,1,0:T(8,128)} %bitcast.4, s32[256,128]{1,0:T(8,128)} %bitcast.6), custom_call_target="tpu_custom_call" | custom-call | tf_op jit(solution)/shard_map/pallas_call | solution.py:392
  1.3 0.0 copy-start
  1.3 3.9 %collective-permute-start = (f32[18,16,128]{2,1,0:T(8,128)S(1)}, f32[18,16,128]{2,1,0:T(8,128)S(1)}, u32[]{:S(2)}, u32[]{:S(2)}) collective-permute-start(f32[18,16,128]{2,1,0:T(8,128)S(1)} %get-tuple-element.27), channel_id=1, source_target_pairs={{0,1},{1,2},{2,3},{3,4},{4,5},{5,6},{6,7},{7,8},{8,9},{9,10},{10,1... | collective-permute-start | bytes 442376 | tf_op jit(solution)/shard_map/ppermute | solution.py:384
  5.2 8.6 %collective-permute-start.1 = (f32[18,16,128]{2,1,0:T(8,128)S(1)}, f32[18,16,128]{2,1,0:T(8,128)S(1)}, u32[]{:S(2)}, u32[]{:S(2)}) collective-permute-start(f32[18,16,128]{2,1,0:T(8,128)S(1)} %get-tuple-element.28), channel_id=1, source_target_pairs={{0,15},{1,0},{2,1},{3,2},{4,3},{5,4},{6,5},{7,6},{8,7},{9,8},{10,9... | collective-permute-start | bytes 442376 | tf_op jit(solution)/shard_map/ppermute | solution.py:385
  13.9 0.6 %collective-permute-done.first.first_y = f32[18,16,128]{2,1,0:T(8,128)S(1)} collective-permute-done((f32[18,16,128]{2,1,0:T(8,128)S(1)}, f32[18,16,128]{2,1,0:T(8,128)S(1)}, u32[]{:S(2)}, u32[]{:S(2)}) %collective-permute-start) | collective-permute-done | bytes 147488 | tf_op jit(solution)/shard_map/ppermute | solution.py:384
  14.4 1.5 %collective-permute-done.1.second.second_y = f32[18,16,128]{2,1,0:T(8,128)S(1)} collective-permute-done((f32[18,16,128]{2,1,0:T(8,128)S(1)}, f32[18,16,128]{2,1,0:T(8,128)S(1)}, u32[]{:S(2)}, u32[]{:S(2)}) %collective-permute-start.1) | collective-permute-done | bytes 147488 | tf_op jit(solution)/shard_map/ppermute | solution.py:385
  15.9 0.2 shard_map.47
  16.1 1.3 %collective-permute-start.2 = (f32[3,384,128]{2,1,0:T(8,128)S(1)}, f32[3,384,128]{2,1,0:T(8,128)S(1)}, u32[]{:S(2)}, u32[]{:S(2)}) collective-permute-start(f32[3,384,128]{2,1,0:T(8,128)S(1)} %get-tuple-element.32), channel_id=1, source_target_pairs={{0,512},{1,513},{2,514},{3,515},{4,516},{5,517},{6,518},{7,519},{8... | collective-permute-start | bytes 1769480 | tf_op jit(solution)/shard_map/ppermute | solution.py:417
  17.4 0.1 shard_map.49
  17.5 11.1 %collective-permute-start.3 = (f32[288,128]{1,0:T(8,128)S(1)}, f32[288,128]{1,0:T(8,128)S(1)}, u32[]{:S(2)}, u32[]{:S(2)}) collective-permute-start(f32[288,128]{1,0:T(8,128)S(1)} %get-tuple-element.34), channel_id=1, source_target_pairs={{0,16},{16,32},{32,48},{48,64},{64,80},{80,96},{96,112},{112,128},... | collective-permute-start | bytes 442376 | tf_op jit(solution)/shard_map/ppermute | solution.py:384
  28.6 9.1 %collective-permute-start.4 = (f32[288,128]{1,0:T(8,128)S(1)}, f32[288,128]{1,0:T(8,128)S(1)}, u32[]{:S(2)}, u32[]{:S(2)}) collective-permute-start(f32[288,128]{1,0:T(8,128)S(1)} %get-tuple-element.35), channel_id=1, source_target_pairs={{0,496},{16,0},{32,16},{48,32},{64,48},{80,64},{96,80},{112,96},{1... | collective-permute-start | bytes 442376 | tf_op jit(solution)/shard_map/ppermute | solution.py:385
  37.7 0.0 collective-permute-done.2.main_a
  37.7 0.0 copy-done
  37.8 4.3 %shard_map.48 = (f32[392,128]{1,0:T(8,128)S(1)}, f32[7,392,128]{2,1,0:T(8,128)S(1)}, f32[4,392,128]{2,1,0:T(8,128)S(1)}, f32[4,256,128]{2,1,0:T(8,128)S(1)}, f32[24,128]{1,0:T(8,128)S(1)}) custom-call(f32[3,256,128]{2,1,0:T(8,128)S(1)} %get-tuple-element.24.w, f32[3,392,128]{2,1,0:T(8,128)S(1)} %get-tuple-element.29.ew, ...), custom_call_target="tpu_custom_call" | custom-call | flops 10000000 | tf_op jit(solution)/shard_map/pallas_call | solution.py:418
  42.1 0.0 collective-permute-done.3.first
  42.1 7.1 %collective-permute-done.4.second = f32[288,128]{1,0:T(8,128)S(1)} collective-permute-done((f32[288,128]{1,0:T(8,128)S(1)}, f32[288,128]{1,0:T(8,128)S(1)}, u32[]{:S(2)}, u32[]{:S(2)}) %collective-permute-start.4) | collective-permute-done | bytes 147488 | tf_op jit(solution)/shard_map/ppermute | solution.py:385
  49.2 1.2 %shard_map.50 = (f32[7,200,128]{2,1,0:T(8,128)S(1)}, f32[4,248,128]{2,1,0:T(8,128)S(1)}, f32[3,288,128]{2,1,0:T(8,128)S(1)}) custom-call(f32[288,128]{1,0:T(8,128)S(1)} %collective-permute-done.3.first, f32[288,128]{1,0:T(8,128)S(1)} %collective-permute-done.4.second, f32[3,392,128]{2,1,0:T(8,128)S(1)} %get-tuple-element.29.ew, ...), custom_call_target="tpu_custom_call" | custom-call | tf_op jit(solution)/shard_map/pallas_call | solution.py:424
  50.4 1.3 %collective-permute-start.5 = (f32[3,288,128]{2,1,0:T(8,128)S(1)}, f32[3,288,128]{2,1,0:T(8,128)S(1)}, u32[]{:S(2)}, u32[]{:S(2)}) collective-permute-start(f32[3,288,128]{2,1,0:T(8,128)S(1)} %get-tuple-element.42), channel_id=1, source_target_pairs={{0,512},{1,513},{2,514},{3,515},{4,516},{5,517},{6,518},{7,519},{8... | collective-permute-start | bytes 1327112 | tf_op jit(solution)/shard_map/ppermute | solution.py:430
  51.7 0.5 shard_map.51.part_edges
  52.2 1.8 %collective-permute-done.5.main_a = f32[3,288,128]{2,1,0:T(8,128)S(1)} collective-permute-done((f32[3,288,128]{2,1,0:T(8,128)S(1)}, f32[3,288,128]{2,1,0:T(8,128)S(1)}, u32[]{:S(2)}, u32[]{:S(2)}) %collective-permute-start.5) | collective-permute-done | bytes 442400 | tf_op jit(solution)/shard_map/ppermute | solution.py:430
  54.1 0.9 %shard_map.52 = f32[4,256,128]{2,1,0:T(8,128)} custom-call(f32[4,256,128]{2,1,0:T(8,128)S(1)} %get-tuple-element.33.part, f32[4,96,128]{2,1,0:T(8,128)S(1)} %shard_map.51.part_edges, f32[7,200,128]{2,1,0:T(8,128)S(1)} %get-tuple-element.41.cf, f32[3,288,128]{2,1,0:T(8,128)S(1)} %collective-permute-done.5.main_a, f32[24,128]{1,0:T(8,128)S(1)} %get-tuple-element.37.table), custom_call_target="tpu_custom_call" | custom-call | tf_op jit(solution)/shard_map/pallas_call | solution.py:432
Async XLA Ops:
  1.3 36.5 %copy-start = (s32[2]{0:T(128)S(1)}, s32[2]{0:T(128)}, u32[]{:S(2)}) copy-start(s32[2]{0:T(128)} %fringe.1) | copy-start | bytes 28
  1.3 13.2 %collective-permute-start = (f32[18,16,128]{2,1,0:T(8,128)S(1)}, f32[18,16,128]{2,1,0:T(8,128)S(1)}, u32[]{:S(2)}, u32[]{:S(2)}) collective-permute-start(f32[18,16,128]{2,1,0:T(8,128)S(1)} %get-tuple-element.27), channel_id=1, source_target_pairs={{0,1},{1,2},{2,3},{3,4},{4,5},{5,6},{6,7},{7,8},{8,9},{9,10},{10,1... | collective-permute-start | bytes 442376 | tf_op jit(solution)/shard_map/ppermute | solution.py:384
  5.2 10.7 %collective-permute-start.1 = (f32[18,16,128]{2,1,0:T(8,128)S(1)}, f32[18,16,128]{2,1,0:T(8,128)S(1)}, u32[]{:S(2)}, u32[]{:S(2)}) collective-permute-start(f32[18,16,128]{2,1,0:T(8,128)S(1)} %get-tuple-element.28), channel_id=1, source_target_pairs={{0,15},{1,0},{2,1},{3,2},{4,3},{5,4},{6,5},{7,6},{8,7},{9,8},{10,9... | collective-permute-start | bytes 442376 | tf_op jit(solution)/shard_map/ppermute | solution.py:385
  16.1 21.6 %collective-permute-start.2 = (f32[3,384,128]{2,1,0:T(8,128)S(1)}, f32[3,384,128]{2,1,0:T(8,128)S(1)}, u32[]{:S(2)}, u32[]{:S(2)}) collective-permute-start(f32[3,384,128]{2,1,0:T(8,128)S(1)} %get-tuple-element.32), channel_id=1, source_target_pairs={{0,512},{1,513},{2,514},{3,515},{4,516},{5,517},{6,518},{7,519},{8... | collective-permute-start | bytes 1769480 | tf_op jit(solution)/shard_map/ppermute | solution.py:417
  17.5 24.6 %collective-permute-start.3 = (f32[288,128]{1,0:T(8,128)S(1)}, f32[288,128]{1,0:T(8,128)S(1)}, u32[]{:S(2)}, u32[]{:S(2)}) collective-permute-start(f32[288,128]{1,0:T(8,128)S(1)} %get-tuple-element.34), channel_id=1, source_target_pairs={{0,16},{16,32},{32,48},{48,64},{64,80},{80,96},{96,112},{112,128},... | collective-permute-start | bytes 442376 | tf_op jit(solution)/shard_map/ppermute | solution.py:384
  28.6 20.6 %collective-permute-start.4 = (f32[288,128]{1,0:T(8,128)S(1)}, f32[288,128]{1,0:T(8,128)S(1)}, u32[]{:S(2)}, u32[]{:S(2)}) collective-permute-start(f32[288,128]{1,0:T(8,128)S(1)} %get-tuple-element.35), channel_id=1, source_target_pairs={{0,496},{16,0},{32,16},{48,32},{64,48},{80,64},{96,80},{112,96},{1... | collective-permute-start | bytes 442376 | tf_op jit(solution)/shard_map/ppermute | solution.py:385
  50.4 3.7 %collective-permute-start.5 = (f32[3,288,128]{2,1,0:T(8,128)S(1)}, f32[3,288,128]{2,1,0:T(8,128)S(1)}, u32[]{:S(2)}, u32[]{:S(2)}) collective-permute-start(f32[3,288,128]{2,1,0:T(8,128)S(1)} %get-tuple-element.42), channel_id=1, source_target_pairs={{0,512},{1,513},{2,514},{3,515},{4,516},{5,517},{6,518},{7,519},{8... | collective-permute-start | bytes 1327112 | tf_op jit(solution)/shard_map/ppermute | solution.py:430

commit v4 on v3

--- a/solution.py
+++ b/solution.py
@@ -134,11 +134,13 @@
     ed[pl.ds(to * R + 3, T), :] = drag_rows(*wind, t[pl.ds(x * T, T), :].astype(F32))
 
 
-def spread_rows(w, a, t, first, second, ew, ea, ed, vel):
+def spread_rows(w, a, t, first, second, main_a, ew, ea, ed, vel):
     for x in range(T):
         own_rows(x, x, w, a, t, ew, ea, ed)
+        for c in range(3):
+            vel[c, pl.ds(x * R, R), :] = jnp.zeros((R, NZ), F32)
+            vel[c, pl.ds(x * R + 3, T), :] = main_a[c, pl.ds(x * T, T), :]
     y_rims(first, second, ew, ea, ed, 0, 0, T)
-    vel[...] = ea[pl.ds(0, 3), pl.ds(0, T * R), :]
 
 
 def nu_rows(ew, at, rows, ones_p, ones_m):
@@ -239,7 +241,7 @@
         out[c, pl.ds(to, T), :] = new[c]
 
 
-def inner(w, ew, ea, ed, main_a, fringe, nu, cf, a1, out, table):
+def inner(w, ew, ea, ed, main_a, fringe, nu, cf, a1, out, table, inside):
     main = is_main()
     fringe_table(fringe, table)
     ones_p, ones_m = edges_z(R)
@@ -265,6 +267,9 @@
         return 0
 
     lax.fori_loop(2, T - 2, plane, 0)
+    for c in range(3):
+        for x in range(2, T - 2):
+            inside[c, pl.ds((x - 2) * T, T), :] = a1[c, pl.ds(x * R + 3, T), :]
     short_p, short_m = edges_z(T)
 
     def later(x, _):
@@ -275,7 +280,7 @@
     lax.fori_loop(3, T - 3, later, 0)
 
 
-def edges(first, second, ew, ea, ed, nu, main_a, table, cf_in, a1_in, cf, a1, sent, sw, sa, sd, sn):
+def edges(first, second, ew, ea, ed, nu, main_a, table, cf_in, a1_in, cf, a1, sent, beside, sw, sa, sd, sn):
     main = is_main()
     for group, shift in zip(KEPT, (LEFT, RIGHT)):
         for x in group:
@@ -333,12 +338,15 @@
             cf[n, pl.ds(p * R, R), :] = cf_in[n, pl.ds(x * R, R), :]
     for c in range(3):
         sent[c, pl.ds(0, T), :] = sa[c, pl.ds(R + 3, T), :]
-        for x in range(T):
-            src = a1[c, pl.ds((x + 1 if x < 8 else x - 7) * R + 3, T), :] if x in (0, 1, 14, 15) else a1_in[
-                c, pl.ds(x * R + 3, T), :
-            ]
-            sent[c, pl.ds((x + 1) * T, T), :] = src
-        sent[c, pl.ds((T + 1) * T, T), :] = sa[c, pl.ds(8 * R + 3, T), :]
+        for k, p in ((1, 1), (2, 2), (3, 7), (4, 8)):
+            sent[c, pl.ds(k * T, T), :] = a1[c, pl.ds(p * R + 3, T), :]
+        sent[c, pl.ds(5 * T, T), :] = sa[c, pl.ds(8 * R + 3, T), :]
+        sent[c, pl.ds(6 * T, T), :] = ea[c, pl.ds(2, T, stride=R), :]
+        sent[c, pl.ds(7 * T, T), :] = ea[c, pl.ds(T + 3, T, stride=R), :]
+    for k, n, row in ((0, 4, 3), (1, 3, T + 2)):
+        beside[k, pl.ds(2, T - 4), :] = cf_in[n, pl.ds(2 * R + row, T - 4, stride=R), :]
+        beside[k, pl.ds(0, 2), :] = cf[n, pl.ds(row, 2, stride=R), :]
+        beside[k, pl.ds(T - 2, 2), :] = cf[n, pl.ds(4 * R + row, 2, stride=R), :]
 
 
 def second_edges(w, a1, cf, part):
@@ -353,26 +361,33 @@
     lax.fori_loop(0, 6, plane, 0)
 
 
-def finish(part, part_edges, cf, main_a, table, out):
+def finish(part, part_edges, cf, beside, inside, main_a, table, out):
     other = 1.0 - is_main()
     for x in range(T):
-        inside = 3 <= x < T - 3
         k = x if x < 8 else x - 10
         rate = rate_rows(table, x, T) * other
-        src, at = (part, x * T) if inside else (part_edges, k * T)
+        src, at = (part, x * T) if 3 <= x < T - 3 else (part_edges, k * T)
         new = [src[c, pl.ds(at, T), :] for c in range(4)]
-        for c in range(3):
-            new[c] = new[c] + rate * main_a[c, pl.ds((x + 1) * T, T), :]
+        push, at = (inside, (x - 2) * T) if 2 <= x < T - 2 else (main_a, (x + 1 if x < 8 else x - 11) * T)
+        for c in range(3):
+            new[c] = new[c] + rate * push[c, pl.ds(at, T), :]
         if x in (0, T - 1):
-            p, n, sign = (0, 2, -1.0) if x == 0 else (T + 1, 1, 1.0)
-            rate = rate_rows(table, p - 1, T) * other
-            beside = [rate * main_a[c, pl.ds(p * T, T), :] for c in range(3)]
+            p, n, sign = (0, 2, -1.0) if x == 0 else (5, 1, 1.0)
+            rate = rate_rows(table, -1 if x == 0 else T, T) * other
+            pushed = [rate * main_a[c, pl.ds(p * T, T), :] for c in range(3)]
             coef = cf[n, pl.ds(k * R + 3, T), :]
             for c in range(3):
-                new[c] = new[c] + coef * beside[c]
-            new[3] = new[3] + (sign * HALF) * beside[0]
+                new[c] = new[c] + coef * pushed[c]
+            new[3] = new[3] + (sign * HALF) * pushed[0]
         for c in range(4):
             out[c, pl.ds(x * T, T), :] = new[c]
+    rate = table[pl.ds(1, T), :] * other
+    for k, y, sign in ((0, 0, -1.0), (1, T - 1, 1.0)):
+        pushed = [rate * main_a[c, pl.ds((6 + k) * T, T), :] for c in range(3)]
+        row = pl.ds(y, T, stride=T)
+        for c in range(3):
+            out[c, row, :] = out[c, row, :] + beside[k] * pushed[c]
+        out[3, row, :] = out[3, row, :] + (sign * HALF) * pushed[1]
 
 
 def ring(axis, by):
@@ -401,6 +416,7 @@
         )
     )
     y1, y2 = exchange(y1, y2, "gy")
+    main_a = lax.ppermute(a, "dom", [(0, 1)])
     x1, x2 = call(
         pack_x,
         (x_msg, x_msg),
@@ -411,25 +427,25 @@
     ew, ea, ed, vel = call(
         spread_rows,
         (shape(*planes(T, 3)), shape(*planes(T, 4)), shape(*planes(T)), shape(3, T * R, NZ)),
-        [VMEM] * 5,
+        [VMEM] * 6,
         flops=10**6,
-    )(w, a, t, y1, y2)
-    main_a = lax.ppermute(vel, "dom", [(0, 1)])
-    nu, cf, a1, part, table = call(
+    )(w, a, t, y1, y2, main_a)
+    nu, cf, a1, part, table, inside = call(
         inner,
-        (shape(*planes(T)), shape(*planes(T, 7)), shape(*planes(T, 4)), tile, shape(R, NZ)),
+        (shape(*planes(T)), shape(*planes(T, 7)), shape(*planes(T, 4)), tile, shape(R, NZ), shape(3, (T - 4) * T, NZ)),
         [VMEM] * 5 + [SMEM],
         flops=10**7,
-    )(w, ew, ea, ed, main_a, fringe_range)
-    cf_edges, a1_edges, sent = call(
+    )(w, ew, ea, ed, vel, fringe_range)
+    inside = lax.ppermute(inside, "dom", [(0, 1)])
+    cf_edges, a1_edges, sent, beside = call(
         edges,
-        (shape(*planes(8, 7)), shape(*planes(10, 4)), shape(3, (T + 2) * T, NZ)),
+        (shape(*planes(8, 7)), shape(*planes(10, 4)), shape(3, 8 * T, NZ), shape(2, T, NZ)),
         [VMEM] * 10,
         scratch=[scratch(*planes(10, 3)), scratch(*planes(10, 4)), scratch(*planes(10)), scratch(*planes(10))],
-    )(x1, x2, ew, ea, ed, nu, main_a, table, cf, a1)
+    )(x1, x2, ew, ea, ed, nu, vel, table, cf, a1)
     main_a1 = lax.ppermute(sent, "dom", [(0, 1)])
     part_edges = call(second_edges, shape(4, 6 * T, NZ), [VMEM] * 3, flops=10**6)(w, a1_edges, cf_edges)
-    out = call(finish, tile, [VMEM] * 5)(part, part_edges, cf_edges, main_a1, table)
+    out = call(finish, tile, [VMEM] * 7)(part, part_edges, cf_edges, beside, inside, main_a1, table)
     return out.reshape(1, 4, T, T, NZ)
 
 

time: 55.2 us -> 54.7 us (level)
  the two profiles are of different devices: /device:TPU:1 before, /device:TPU:7 now
where the time goes in v4:
time: 54.7 us; the launch traced here: 54.5 us
  starting transfers between devices  31.6 us (58%)
  waiting for transfers between devices  14.3 us (26%)
  Pallas kernels  8.52 us (16%)
    ppermute x2, starting transfers between devices, exchange(): first = lax.ppermute(first, axis, ring(axis, 1))  14.6 us
    ppermute x2, starting transfers between devices, exchange(): second = lax.ppermute(second, axis, ring(axis, -1))  13.1 us
    ppermute x2, waiting for transfers between devices, exchange(): second = lax.ppermute(second, axis, ring(axis, -1))  8.96 us
    ppermute x1, waiting for transfers between devices, on_device(): main_a1 = lax.ppermute(sent, 'dom', [(0, 1)])  5.14 us
    pallas_call x1, Pallas kernels, on_device(): call(inner, (shape(*planes(T)), shape(*planes(T, 7)), shape(*planes(T, 4)...  4.34 us
    ppermute x1, starting transfers between devices, on_device(): main_a = lax.ppermute(a, 'dom', [(0, 1)])  1.29 us
    ppermute x1, starting transfers between devices, on_device(): inside = lax.ppermute(inside, 'dom', [(0, 1)])  1.29 us
    ppermute x1, starting transfers between devices, on_device(): main_a1 = lax.ppermute(sent, 'dom', [(0, 1)])  1.29 us
  transfers between devices with their start and end apart: 7, of which 4 were waited for; matrix products, arithmetic and copies ran while one was open for 0% of the time, Pallas kernels for 12%

profile of v4, /device:TPU:7, one launch (start us, length us, event | category | flops | bytes accessed | tf_op | source)
XLA Modules:
  0.0 54.5 jit_solution(5372423992727648872)
XLA Ops:
  0.0 1.3 %shard_map.46 = (f32[18,16,128]{2,1,0:T(8,128)S(1)}, f32[18,16,128]{2,1,0:T(8,128)S(1)}, f32[3,256,128]{2,1,0:T(8,128)S(1)}, f32[4,256,128]{2,1,0:T(8,128)S(1)}, s32[256,128]{1,0:T(8,128)S(1)}) custom-call(f32[3,256,128]{2,1,0:T(8,128)} %bitcast.5, f32[4,256,128]{2,1,0:T(8,128)} %bitcast.4, s32[256,128]{1,0:T(8,128)} %bitcast.6), custom_call_target="tpu_custom_call" | custom-call | tf_op jit(solution)/shard_map/pallas_call | solution.py:407
  1.3 1.3 %collective-permute-start.2 = (f32[4,256,128]{2,1,0:T(8,128)S(1)}, f32[4,256,128]{2,1,0:T(8,128)S(1)}, u32[]{:S(2)}, u32[]{:S(2)}) collective-permute-start(f32[4,256,128]{2,1,0:T(8,128)S(1)} %get-tuple-element.27.a), channel_id=1, source_target_pairs={{0,512},{1,513},{2,514},{3,515},{4,516},{5,517},{6,518},{7,519},{8... | collective-permute-start | bytes 1572872 | tf_op jit(solution)/shard_map/ppermute | solution.py:419
  2.6 3.9 %collective-permute-start = (f32[18,16,128]{2,1,0:T(8,128)S(1)}, f32[18,16,128]{2,1,0:T(8,128)S(1)}, u32[]{:S(2)}, u32[]{:S(2)}) collective-permute-start(f32[18,16,128]{2,1,0:T(8,128)S(1)} %get-tuple-element.29), channel_id=1, source_target_pairs={{0,1},{1,2},{2,3},{3,4},{4,5},{5,6},{6,7},{7,8},{8,9},{9,10},{10,1... | collective-permute-start | bytes 442376 | tf_op jit(solution)/shard_map/ppermute | solution.py:399
  6.5 1.9 %collective-permute-start.1 = (f32[18,16,128]{2,1,0:T(8,128)S(1)}, f32[18,16,128]{2,1,0:T(8,128)S(1)}, u32[]{:S(2)}, u32[]{:S(2)}) collective-permute-start(f32[18,16,128]{2,1,0:T(8,128)S(1)} %get-tuple-element.30), channel_id=1, source_target_pairs={{0,15},{1,0},{2,1},{3,2},{4,3},{5,4},{6,5},{7,6},{8,7},{9,8},{10,9... | collective-permute-start | bytes 442376 | tf_op jit(solution)/shard_map/ppermute | solution.py:400
  8.4 0.2 collective-permute-done.first.first_y
  8.6 5.9 %collective-permute-done.1.second.second_y = f32[18,16,128]{2,1,0:T(8,128)S(1)} collective-permute-done((f32[18,16,128]{2,1,0:T(8,128)S(1)}, f32[18,16,128]{2,1,0:T(8,128)S(1)}, u32[]{:S(2)}, u32[]{:S(2)}) %collective-permute-start.1) | collective-permute-done | bytes 147488 | tf_op jit(solution)/shard_map/ppermute | solution.py:400
  14.5 0.0 copy-start
  14.5 0.1 shard_map.49
  14.6 10.6 %collective-permute-start.3 = (f32[288,128]{1,0:T(8,128)S(1)}, f32[288,128]{1,0:T(8,128)S(1)}, u32[]{:S(2)}, u32[]{:S(2)}) collective-permute-start(f32[288,128]{1,0:T(8,128)S(1)} %get-tuple-element.36), channel_id=1, source_target_pairs={{0,16},{16,32},{32,48},{48,64},{64,80},{80,96},{96,112},{112,128},... | collective-permute-start | bytes 442376 | tf_op jit(solution)/shard_map/ppermute | solution.py:399
  25.3 11.2 %collective-permute-start.4 = (f32[288,128]{1,0:T(8,128)S(1)}, f32[288,128]{1,0:T(8,128)S(1)}, u32[]{:S(2)}, u32[]{:S(2)}) collective-permute-start(f32[288,128]{1,0:T(8,128)S(1)} %get-tuple-element.37), channel_id=1, source_target_pairs={{0,496},{16,0},{32,16},{48,32},{64,48},{80,64},{96,80},{112,96},{1... | collective-permute-start | bytes 442376 | tf_op jit(solution)/shard_map/ppermute | solution.py:400
  36.5 0.0 collective-permute-done.2.main_a
  36.5 0.2 shard_map.47
  36.7 0.0 copy-done
  36.7 4.3 %shard_map.48 = (f32[392,128]{1,0:T(8,128)S(1)}, f32[7,392,128]{2,1,0:T(8,128)S(1)}, f32[4,392,128]{2,1,0:T(8,128)S(1)}, f32[4,256,128]{2,1,0:T(8,128)S(1)}, f32...) custom-call(f32[3,256,128]{2,1,0:T(8,128)S(1)} %get-tuple-element.26.w, f32[3,392,128]{2,1,0:T(8,128)S(1)} %get-tuple-element.31.ew, ...), custom_call_target="tpu_custom_call" | custom-call | flops 10000000 | tf_op jit(solution)/shard_map/pallas_call | solution.py:433
  41.0 1.3 %collective-permute-start.5 = (f32[3,192,128]{2,1,0:T(8,128)S(1)}, f32[3,192,128]{2,1,0:T(8,128)S(1)}, u32[]{:S(2)}, u32[]{:S(2)}) collective-permute-start(f32[3,192,128]{2,1,0:T(8,128)S(1)} %get-tuple-element.45), channel_id=1, source_target_pairs={{0,512},{1,513},{2,514},{3,515},{4,516},{5,517},{6,518},{7,519},{8... | collective-permute-start | bytes 884744 | tf_op jit(solution)/shard_map/ppermute | solution.py:439
  42.3 0.0 collective-permute-done.3.first
  42.3 3.0 %collective-permute-done.4.second = f32[288,128]{1,0:T(8,128)S(1)} collective-permute-done((f32[288,128]{1,0:T(8,128)S(1)}, f32[288,128]{1,0:T(8,128)S(1)}, u32[]{:S(2)}, u32[]{:S(2)}) %collective-permute-start.4) | collective-permute-done | bytes 147488 | tf_op jit(solution)/shard_map/ppermute | solution.py:400
  45.4 1.2 %shard_map.50 = (f32[7,200,128]{2,1,0:T(8,128)S(1)}, f32[4,248,128]{2,1,0:T(8,128)S(1)}, f32[3,128,128]{2,1,0:T(8,128)S(1)}, f32[2,16,128]{2,1,0:T(8,128)S(1)}) custom-call(f32[288,128]{1,0:T(8,128)S(1)} %collective-permute-done.3.first, f32[288,128]{1,0:T(8,128)S(1)} %collective-permute-done.4.second, f32[3,392,128]{2,1,0:T(8,128)S(1)} %get-tuple-element.31.ew, ...), custom_call_target="tpu_custom_call" | custom-call | tf_op jit(solution)/shard_map/pallas_call | solution.py:440
  46.6 1.3 %collective-permute-start.6 = (f32[3,128,128]{2,1,0:T(8,128)S(1)}, f32[3,128,128]{2,1,0:T(8,128)S(1)}, u32[]{:S(2)}, u32[]{:S(2)}) collective-permute-start(f32[3,128,128]{2,1,0:T(8,128)S(1)} %get-tuple-element.46), channel_id=1, source_target_pairs={{0,512},{1,513},{2,514},{3,515},{4,516},{5,517},{6,518},{7,519},{8... | collective-permute-start | bytes 589832 | tf_op jit(solution)/shard_map/ppermute | solution.py:446
  47.9 0.5 shard_map.51.part_edges
  48.4 5.1 %collective-permute-done.6.main_a = f32[3,128,128]{2,1,0:T(8,128)S(1)} collective-permute-done((f32[3,128,128]{2,1,0:T(8,128)S(1)}, f32[3,128,128]{2,1,0:T(8,128)S(1)}, u32[]{:S(2)}, u32[]{:S(2)}) %collective-permute-start.6) | collective-permute-done | bytes 196640 | tf_op jit(solution)/shard_map/ppermute | solution.py:446
  53.5 0.0 collective-permute-done.5.inside
  53.5 0.9 %shard_map.52 = f32[4,256,128]{2,1,0:T(8,128)} custom-call(f32[4,256,128]{2,1,0:T(8,128)S(1)} %get-tuple-element.35.part, f32[4,96,128]{2,1,0:T(8,128)S(1)} %shard_map.51.part_edges, f32[7,200,128]{2,1,0:T(8,128)S(1)} %get-tuple-element.43.cf, f32[2,16,128]{2,1,0:T(8,128)S(1)} %get-tuple-element.44.beside, f32[3,192,128]{2,1,0:T(8,128)S(1)} %collective-permute-done.5.inside, ...), custom_call_target="tpu_custom_call" | custom-call | tf_op jit(solution)/shard_map/pallas_call | solution.py:448
Async XLA Ops:
  1.3 35.2 %collective-permute-start.2 = (f32[4,256,128]{2,1,0:T(8,128)S(1)}, f32[4,256,128]{2,1,0:T(8,128)S(1)}, u32[]{:S(2)}, u32[]{:S(2)}) collective-permute-start(f32[4,256,128]{2,1,0:T(8,128)S(1)} %get-tuple-element.27.a), channel_id=1, source_target_pairs={{0,512},{1,513},{2,514},{3,515},{4,516},{5,517},{6,518},{7,519},{8... | collective-permute-start | bytes 1572872 | tf_op jit(solution)/shard_map/ppermute | solution.py:419
  2.6 6.0 %collective-permute-start = (f32[18,16,128]{2,1,0:T(8,128)S(1)}, f32[18,16,128]{2,1,0:T(8,128)S(1)}, u32[]{:S(2)}, u32[]{:S(2)}) collective-permute-start(f32[18,16,128]{2,1,0:T(8,128)S(1)} %get-tuple-element.29), channel_id=1, source_target_pairs={{0,1},{1,2},{2,3},{3,4},{4,5},{5,6},{6,7},{7,8},{8,9},{9,10},{10,1... | collective-permute-start | bytes 442376 | tf_op jit(solution)/shard_map/ppermute | solution.py:399
  6.5 8.0 %collective-permute-start.1 = (f32[18,16,128]{2,1,0:T(8,128)S(1)}, f32[18,16,128]{2,1,0:T(8,128)S(1)}, u32[]{:S(2)}, u32[]{:S(2)}) collective-permute-start(f32[18,16,128]{2,1,0:T(8,128)S(1)} %get-tuple-element.30), channel_id=1, source_target_pairs={{0,15},{1,0},{2,1},{3,2},{4,3},{5,4},{6,5},{7,6},{8,7},{9,8},{10,9... | collective-permute-start | bytes 442376 | tf_op jit(solution)/shard_map/ppermute | solution.py:400
  14.5 22.2 %copy-start = (s32[2]{0:T(128)S(1)}, s32[2]{0:T(128)}, u32[]{:S(2)}) copy-start(s32[2]{0:T(128)} %fringe.1) | copy-start | bytes 28
  14.6 27.7 %collective-permute-start.3 = (f32[288,128]{1,0:T(8,128)S(1)}, f32[288,128]{1,0:T(8,128)S(1)}, u32[]{:S(2)}, u32[]{:S(2)}) collective-permute-start(f32[288,128]{1,0:T(8,128)S(1)} %get-tuple-element.36), channel_id=1, source_target_pairs={{0,16},{16,32},{32,48},{48,64},{64,80},{80,96},{96,112},{112,128},... | collective-permute-start | bytes 442376 | tf_op jit(solution)/shard_map/ppermute | solution.py:399
  25.3 20.1 %collective-permute-start.4 = (f32[288,128]{1,0:T(8,128)S(1)}, f32[288,128]{1,0:T(8,128)S(1)}, u32[]{:S(2)}, u32[]{:S(2)}) collective-permute-start(f32[288,128]{1,0:T(8,128)S(1)} %get-tuple-element.37), channel_id=1, source_target_pairs={{0,496},{16,0},{32,16},{48,32},{64,48},{80,64},{96,80},{112,96},{1... | collective-permute-start | bytes 442376 | tf_op jit(solution)/shard_map/ppermute | solution.py:400
  41.0 12.5 %collective-permute-start.5 = (f32[3,192,128]{2,1,0:T(8,128)S(1)}, f32[3,192,128]{2,1,0:T(8,128)S(1)}, u32[]{:S(2)}, u32[]{:S(2)}) collective-permute-start(f32[3,192,128]{2,1,0:T(8,128)S(1)} %get-tuple-element.45), channel_id=1, source_target_pairs={{0,512},{1,513},{2,514},{3,515},{4,516},{5,517},{6,518},{7,519},{8... | collective-permute-start | bytes 884744 | tf_op jit(solution)/shard_map/ppermute | solution.py:439
  46.6 7.0 %collective-permute-start.6 = (f32[3,128,128]{2,1,0:T(8,128)S(1)}, f32[3,128,128]{2,1,0:T(8,128)S(1)}, u32[]{:S(2)}, u32[]{:S(2)}) collective-permute-start(f32[3,128,128]{2,1,0:T(8,128)S(1)} %get-tuple-element.46), channel_id=1, source_target_pairs={{0,512},{1,513},{2,514},{3,515},{4,516},{5,517},{6,518},{7,519},{8... | collective-permute-start | bytes 589832 | tf_op jit(solution)/shard_map/ppermute | solution.py:446
